TPU v7x, 512 devices: a whole 4x4x16 slice. The times are simulated.
512 devices in a mesh: rep: 2 (over core), ep: 64 (over z, y), dp: 4 (over x).
Axes of the slice: x: 4, y: 4, z: 16, core: 2. Of those that a mesh axis runs over, the one named last changes fastest.
Arguments:
- tokens: bfloat16 [16384, 2048], P(('rep', 'ep', 'dp')), may hold values from -6 to 6
- upstream: bfloat16 [16384, 2048], P(('rep', 'ep', 'dp')), may hold values from -6 to 6
- expert_ids: int32 [16384, 4], P(('rep', 'ep', 'dp')), may hold values from 0 to 63, all different within a row; in each aligned block of 32 rows (0 to 31, 32 to 63, ...) at most 4 rows name the same one
- route_weight: bfloat16 [16384, 4], P(('rep', 'ep', 'dp')), may hold values from 0.099609375 to 1
- gate_weight: bfloat16 [64, 384, 2048], P('ep', 'dp'), may hold values from -0.125 to 0.125
- up_weight: bfloat16 [64, 384, 2048], P('ep', 'dp'), may hold values from -0.125 to 0.125
- down_weight: bfloat16 [64, 384, 2048], P('ep', 'dp'), may hold values from -0.3125 to 0.3125
Outputs:
- d_tokens: bfloat16 [16384, 2048], P(('rep', 'ep', 'dp'))
- d_probs: bfloat16 [16384, 4], P(('rep', 'ep', 'dp'))
- grad_down: float32 [64, 384, 2048], P('ep', 'dp')
Inputs may be any that keep to these rules, and one draw needn't show every extreme that they name: `expert_ids`: each row names 4 different experts; among the rows of one device no expert is named by more than 4 rows, and in every draw some expert is named by exactly 4 rows of some device.
All inputs are finite; a program needn't handle non-finite values.
Results may differ from a plain program's by a relative error of at most 0.012.
Values may be sent and summed in bfloat16 or wider, within the bound.
A program may use at most 64 MiB of HBM per device.

v0:
```python
import jax
import jax.numpy as jnp
from jax import lax
from jax.sharding import PartitionSpec as P


def contract_last(left, right):
    return lax.dot_general(
        left, right, (((1,), (1,)), ((), ())), preferred_element_type=jnp.float32
    )


def local(tokens, upstream, expert_ids, route_weight, gate_weight, up_weight, down_weight):
    tok_dev, model_width = tokens.shape
    top_count = expert_ids.shape[1]
    experts = lax.axis_size("ep")
    capacity = 2 * ((5 * tok_dev * top_count + 8 * experts - 1) // (8 * experts))
    route_count = tok_dev * top_count
    flat_ids = expert_ids.reshape(route_count)
    onehot = (flat_ids[:, None] == jnp.arange(experts, dtype=jnp.int32)[None, :]).astype(jnp.int32)
    before = jnp.cumsum(onehot, axis=0) - onehot
    rank_in = jnp.sum(before * onehot, axis=1)
    slot_index = flat_ids * capacity + rank_in
    slot_count = experts * capacity
    owner = (
        jnp.full((slot_count,), route_count, jnp.int32)
        .at[slot_index]
        .set(jnp.arange(route_count, dtype=jnp.int32))
    )
    is_valid = owner < route_count
    owner_safe = jnp.minimum(owner, route_count - 1)
    token_row = owner_safe // top_count
    x_send = jnp.where(is_valid[:, None], tokens[token_row], jnp.zeros((), tokens.dtype)).reshape(
        experts, capacity, model_width
    )
    dy_send = jnp.where(
        is_valid[:, None], upstream[token_row], jnp.zeros((), upstream.dtype)
    ).reshape(experts, capacity, model_width)
    weight_send = jnp.where(
        is_valid, route_weight.reshape(route_count)[owner_safe], jnp.zeros((), route_weight.dtype)
    ).reshape(experts, capacity)
    arrived = (
        lax.all_to_all(x_send, "ep", split_axis=0, concat_axis=0, tiled=True),
        lax.all_to_all(dy_send, "ep", split_axis=0, concat_axis=0, tiled=True),
        lax.all_to_all(weight_send, "ep", split_axis=0, concat_axis=0, tiled=True),
    )
    x_rows = arrived[0].reshape(slot_count, model_width)
    dy_rows = arrived[1].reshape(slot_count, model_width)
    weight_rows = arrived[2].reshape(slot_count)
    d_out = (weight_rows.astype(jnp.float32)[:, None] * dy_rows.astype(jnp.float32)).astype(
        jnp.bfloat16
    )
    gate_piece = lax.all_gather(gate_weight, "dp", axis=1, tiled=True)[0]
    up_piece = lax.all_gather(up_weight, "dp", axis=1, tiled=True)[0]
    down_piece = lax.all_gather(down_weight, "dp", axis=1, tiled=True)[0]
    gate_pre = contract_last(x_rows, gate_piece)
    up_pre = contract_last(x_rows, up_piece)
    sig_gate = jax.nn.sigmoid(gate_pre)
    silu_gate = gate_pre * sig_gate
    act_rows = (silu_gate * up_pre).astype(jnp.bfloat16)
    out_sum = jnp.dot(act_rows, down_piece, preferred_element_type=jnp.float32)
    d_act = contract_last(d_out, down_piece)
    d_gate = (d_act * up_pre * sig_gate * (1.0 + gate_pre * (1.0 - sig_gate))).astype(jnp.bfloat16)
    d_up = (d_act * silu_gate).astype(jnp.bfloat16)
    dx_sum = jnp.dot(d_gate, gate_piece, preferred_element_type=jnp.float32)
    dx_sum = dx_sum + jnp.dot(d_up, up_piece, preferred_element_type=jnp.float32)
    grad_piece = lax.dot_general(
        act_rows, d_out, (((0,), (0,)), ((), ())), preferred_element_type=jnp.float32
    )
    grad_full = grad_piece
    out_sum, dx_sum, grad_full = (out_sum, dx_sum, grad_full)
    dprob_rows = (
        jnp.sum(dy_rows.astype(jnp.float32) * out_sum, axis=-1)
        .astype(jnp.bfloat16)
        .reshape(experts, capacity)
    )
    dx_rows = dx_sum.astype(jnp.bfloat16).reshape(experts, capacity, model_width)
    returned = (
        lax.all_to_all(dx_rows, "ep", split_axis=0, concat_axis=0, tiled=True),
        lax.all_to_all(dprob_rows, "ep", split_axis=0, concat_axis=0, tiled=True),
    )
    dx_slots = returned[0].reshape(slot_count, model_width)
    dprob_slots = returned[1].reshape(slot_count)
    route_dx = dx_slots[slot_index].astype(jnp.float32).reshape(tok_dev, top_count, model_width)
    d_tokens = jnp.sum(route_dx, axis=1).astype(jnp.bfloat16)
    d_probs = dprob_slots[slot_index].reshape(tok_dev, top_count)
    grad_shard = lax.psum_scatter(
        grad_full.astype(jnp.bfloat16), "dp", scatter_dimension=0, tiled=True
    )
    grad_total = lax.psum(grad_shard, "rep").astype(jnp.float32)
    return (d_tokens, d_probs, grad_total[None])


def solution(mesh):
    placed = (
        P(("rep", "ep", "dp"), None),
        P(("rep", "ep", "dp"), None),
        P(("rep", "ep", "dp"), None),
        P(("rep", "ep", "dp"), None),
        P("ep", "dp", None),
        P("ep", "dp", None),
        P("ep", "dp", None),
    )
    return jax.shard_map(
        local,
        mesh=mesh,
        in_specs=placed,
        out_specs=(P(("rep", "ep", "dp"), None), P(("rep", "ep", "dp"), None), P("ep", "dp", None)),
        check_vma=False,
    )
```

profile of v0, /device:TPU:1, one launch (start us, length us, event | category | flops | bytes accessed | tf_op | source)
XLA Modules:
  0.0 322.0 jit_solution(5766718910639316087)
XLA Ops:
  11.3 1.9 gather_fusion
  14.0 19.3 %all-to-all-start = ((bf16[64,1,4]{2,1,0:T(2,128)(2,1)}), bf16[64,1,4]{2,1,0:T(2,128)(2,1)S(1)}, u32[]{:S(2)}, u32[]{:S(2)}) async-start(bf16[64,1,4]{2,1,0:T(2,128)(2,1)} %all_to_all.25), calls=%async_computation | async-start | bytes 65536 | tf_op jit(solution)/shard_map/all_to_all | solution.py:45
  33.4 1.4 gather_fusion.2
  35.7 1.4 gather_fusion.1
  37.5 2.4 broadcast_select_fusion.1
  39.8 6.8 %all-to-all-done = bf16[64,1,4]{2,1,0:T(2,128)(2,1)S(1)} async-done(((bf16[64,1,4]{2,1,0:T(2,128)(2,1)}), bf16[64,1,4]{2,1,0:T(2,128)(2,1)S(1)}, u32[]{:S(2)}, u32[]{:S(2)}) %all-to-all-start) | async-done | bytes 544 | tf_op jit(solution)/shard_map/all_to_all | solution.py:45
  46.7 7.7 %all-to-all-start.1 = ((bf16[64,4,2048]{2,1,0:T(4,128)(2,1)}), bf16[64,4,2048]{2,1,0:T(4,128)(2,1)S(1)}, u32[]{:S(2)}, u32[]{:S(2)}) async-start(bf16[64,4,2048]{2,1,0:T(4,128)(2,1)} %get-tuple-element.14), calls=%async_computation.1 | async-start | bytes 2097152 | tf_op jit(solution)/shard_map/all_to_all | solution.py:44
  55.1 50.5 %all-to-all-done.1 = bf16[64,4,2048]{2,1,0:T(4,128)(2,1)S(1)} async-done(((bf16[64,4,2048]{2,1,0:T(4,128)(2,1)}), bf16[64,4,2048]{2,1,0:T(4,128)(2,1)S(1)}, u32[]{:S(2)}, u32[]{:S(2)}) %all-to-all-start.1) | async-done | bytes 1048608 | tf_op jit(solution)/shard_map/all_to_all | solution.py:44
  105.6 9.1 %all-to-all-start.2 = ((bf16[64,4,2048]{2,1,0:T(4,128)(2,1)}), bf16[64,4,2048]{2,1,0:T(4,128)(2,1)}, u32[]{:S(2)}, u32[]{:S(2)}) async-start(bf16[64,4,2048]{2,1,0:T(4,128)(2,1)} %get-tuple-element.15), calls=%async_computation.2 | async-start | bytes 2097152 | tf_op jit(solution)/shard_map/all_to_all | solution.py:43
  118.0 47.9 %all-to-all-done.2 = bf16[64,4,2048]{2,1,0:T(4,128)(2,1)} async-done(((bf16[64,4,2048]{2,1,0:T(4,128)(2,1)}), bf16[64,4,2048]{2,1,0:T(4,128)(2,1)}, u32[]{:S(2)}, u32[]{:S(2)}) %all-to-all-start.2) | async-done | bytes 1048608 | tf_op jit(solution)/shard_map/all_to_all | solution.py:43
  165.8 1.3 reshape.112
  167.2 2.9 fusion.3
  170.1 3.0 multiply_convert_fusion.3
  173.1 17.0 %all-gather.4.cloned.1.call-done = bf16[1,384,2048]{2,1,0:T(8,128)(2,1)} async-done(((bf16[1,96,2048]{2,1,0:T(8,128)(2,1)}), bf16[1,384,2048]{2,1,0:T(8,128)(2,1)}) %all-gather.4.cloned.1.call-update) | async-done | bytes 1572880 | tf_op jit(solution)/shard_map/all_gather | solution.py:55
  190.0 2.3 fusion.11
  193.1 15.5 %all-to-all-start.4 = ((bf16[64,1,4]{2,1,0:T(2,128)(2,1)}), bf16[64,1,4]{2,1,0:T(2,128)(2,1)S(1)}, u32[]{:S(2)}, u32[]{:S(2)}) async-start(bf16[64,1,4]{2,1,0:T(2,128)(2,1)} %convert_element_type.91), calls=%async_computation.4 | async-start | bytes 65536 | tf_op jit(solution)/shard_map/all_to_all | solution.py:80
  208.7 2.3 fusion.9
  214.4 7.5 %all-to-all-done.4 = bf16[64,1,4]{2,1,0:T(2,128)(2,1)S(1)} async-done(((bf16[64,1,4]{2,1,0:T(2,128)(2,1)}), bf16[64,1,4]{2,1,0:T(2,128)(2,1)S(1)}, u32[]{:S(2)}, u32[]{:S(2)}) %all-to-all-start.4) | async-done | bytes 544 | tf_op jit(solution)/shard_map/all_to_all | solution.py:80
  221.9 7.1 %all-to-all-start.3 = ((bf16[64,4,2048]{2,1,0:T(4,128)(2,1)}), bf16[64,4,2048]{2,1,0:T(4,128)(2,1)}, u32[]{:S(2)}, u32[]{:S(2)}) async-start(bf16[64,4,2048]{2,1,0:T(4,128)(2,1)} %reshape.113), calls=%async_computation.3 | async-start | bytes 2097152 | tf_op jit(solution)/shard_map/all_to_all | solution.py:79
  229.2 1.8 convolution_convert_fusion
  231.1 34.1 %reduce-scatter.2.cloned.1.call-done = bf16[96,2048]{1,0:T(8,128)(2,1)} async-done(((bf16[384,2048]{1,0:T(8,128)(2,1)}), bf16[96,2048]{1,0:T(8,128)(2,1)}) %reduce-scatter.2.cloned.1.call-update) | async-done | bytes 393232 | tf_op jit(solution)/shard_map/reduce_scatter | solution.py:87
  267.5 42.2 %all-reduce.2.cloned.1.call-done = bf16[1,96,2048]{2,1,0:T(8,128)(2,1)} async-done(((bf16[1,96,2048]{2,1,0:T(8,128)(2,1)}), bf16[1,96,2048]{2,1,0:T(8,128)(2,1)}) %all-reduce.2.cloned.1.call-update) | async-done | bytes 393232 | tf_op jit(solution)/shard_map/psum | solution.py:90
  309.7 1.9 broadcast_in_dim.49
  311.7 1.3 reshape.114
  (66 shorter events, 19.4 us)
Async XLA Ops:
  7.2 26.2 %copy-start = (bf16[32,2048]{1,0:T(8,128)(2,1)S(1)}, bf16[32,2048]{1,0:T(8,128)(2,1)}, u32[]{:S(2)}) copy-start(bf16[32,2048]{1,0:T(8,128)(2,1)} %param.7) | copy-start | bytes 393220
  14.0 32.7 %all-to-all-start = ((bf16[64,1,4]{2,1,0:T(2,128)(2,1)}), bf16[64,1,4]{2,1,0:T(2,128)(2,1)S(1)}, u32[]{:S(2)}, u32[]{:S(2)}) async-start(bf16[64,1,4]{2,1,0:T(2,128)(2,1)} %all_to_all.25), calls=%async_computation | async-start | bytes 65536 | tf_op jit(solution)/shard_map/all_to_all | solution.py:45
  34.7 0.9 copy-start.1
  46.7 58.9 %all-to-all-start.1 = ((bf16[64,4,2048]{2,1,0:T(4,128)(2,1)}), bf16[64,4,2048]{2,1,0:T(4,128)(2,1)S(1)}, u32[]{:S(2)}, u32[]{:S(2)}) async-start(bf16[64,4,2048]{2,1,0:T(4,128)(2,1)} %get-tuple-element.14), calls=%async_computation.1 | async-start | bytes 2097152 | tf_op jit(solution)/shard_map/all_to_all | solution.py:44
  54.4 112.8 %all-gather.8.cloned.1.call-start = ((), (), s32[]{:S(2)}) async-start(), calls=%async_computation.8 | async-start | bytes 1966080 | tf_op jit(solution)/shard_map/all_gather | solution.py:53
  105.6 60.3 %all-to-all-start.2 = ((bf16[64,4,2048]{2,1,0:T(4,128)(2,1)}), bf16[64,4,2048]{2,1,0:T(4,128)(2,1)}, u32[]{:S(2)}, u32[]{:S(2)}) async-start(bf16[64,4,2048]{2,1,0:T(4,128)(2,1)} %get-tuple-element.15), calls=%async_computation.2 | async-start | bytes 2097152 | tf_op jit(solution)/shard_map/all_to_all | solution.py:43
  114.7 55.4 %all-gather.6.cloned.1.call-start = ((), (), s32[]{:S(2)}) async-start(), calls=%async_computation.7 | async-start | bytes 1966080 | tf_op jit(solution)/shard_map/all_gather | solution.py:54
  115.4 74.6 %all-gather.4.cloned.1.call-start = ((), (), s32[]{:S(2)}) async-start(), calls=%async_computation.6 | async-start | bytes 1966080 | tf_op jit(solution)/shard_map/all_gather | solution.py:55
  190.0 18.6 %copy-start.3 = (bf16[256,2048]{1,0:T(8,128)(2,1)S(1)}, bf16[256,2048]{1,0:T(8,128)(2,1)}, u32[]{:S(2)}) copy-start(bf16[256,2048]{1,0:T(8,128)(2,1)} %convert_element_type.75) | copy-start | bytes 3145732
  193.1 28.8 %all-to-all-start.4 = ((bf16[64,1,4]{2,1,0:T(2,128)(2,1)}), bf16[64,1,4]{2,1,0:T(2,128)(2,1)S(1)}, u32[]{:S(2)}, u32[]{:S(2)}) async-start(bf16[64,1,4]{2,1,0:T(2,128)(2,1)} %convert_element_type.91), calls=%async_computation.4 | async-start | bytes 65536 | tf_op jit(solution)/shard_map/all_to_all | solution.py:80
  208.6 2.3 copy-start.2
  208.6 2.3 copy-start.4
  208.6 2.3 copy-start.6
  211.0 1.4 copy-start.5
  221.9 89.8 %all-to-all-start.3 = ((bf16[64,4,2048]{2,1,0:T(4,128)(2,1)}), bf16[64,4,2048]{2,1,0:T(4,128)(2,1)}, u32[]{:S(2)}, u32[]{:S(2)}) async-start(bf16[64,4,2048]{2,1,0:T(4,128)(2,1)} %reshape.113), calls=%async_computation.3 | async-start | bytes 2097152 | tf_op jit(solution)/shard_map/all_to_all | solution.py:79
  229.0 36.3 %reduce-scatter.2.cloned.1.call-start = ((), (), s32[]{:S(2)}) async-start(), calls=%async_computation.9 | async-start | bytes 1966080 | tf_op jit(solution)/shard_map/reduce_scatter | solution.py:87
  231.1 78.6 %all-reduce.2.cloned.1.call-start = ((), (), s32[]{:S(2)}) async-start(), calls=%async_computation.10 | async-start | bytes 786432 | tf_op jit(solution)/shard_map/psum | solution.py:90
Sparse Core Ops, SparseCore 0:
  57.3 35.5 all-gather.7
  117.6 36.0 all-gather.5
  155.8 34.1 all-gather.3
  232.3 32.8 reduce-scatter.1
  268.0 41.6 all-reduce.1
where the time goes:
time: 323 us; the launch traced here: 322 us
  waiting for transfers between devices  208 us (64%)
  starting transfers between devices  58.9 us (18%)
  local copies, waits for them, and re-layouts  19.6 us (6%)
  between operations  14.1 us (4%)
  matrix products  13.8 us (4%)
  other arithmetic  7.56 us (2%)
    all_to_all x1, waiting for transfers between devices, local(): lax.all_to_all(dy_send, 'ep', split_axis=0, concat_axis=0, tiled=True)  50.5 us
    all_to_all x1, waiting for transfers between devices, local(): lax.all_to_all(x_send, 'ep', split_axis=0, concat_axis=0, tiled=True)  47.9 us
    psum x1, waiting for transfers between devices, local(): grad_total = lax.psum(grad_shard, 'rep').astype(jnp.float32)  42.2 us
    reduce_scatter x1, waiting for transfers between devices, local(): lax.psum_scatter(grad_full.astype(jnp.bfloat16), 'dp', scatter_dimension=...  34.1 us
    all_to_all x1, starting transfers between devices, local(): lax.all_to_all(weight_send, 'ep', split_axis=0, concat_axis=0, tiled=True)  19.3 us
    all_gather x1, waiting for transfers between devices, local(): down_piece = lax.all_gather(down_weight, 'dp', axis=1, tiled=True)[0]  17 us
    all_to_all x1, starting transfers between devices, local(): lax.all_to_all(dprob_rows, 'ep', split_axis=0, concat_axis=0, tiled=True)  15.5 us
    all_to_all x1, starting transfers between devices, local(): lax.all_to_all(x_send, 'ep', split_axis=0, concat_axis=0, tiled=True)  9.08 us
  transfers between devices with their start and end apart: 10, of which 7 were waited for; matrix products, arithmetic and copies ran while one was open for 8% of the time, Pallas kernels for 0%

commit v1 on v0

v1 whole, which is shorter than its diff:
```python
import functools

import jax
import jax.numpy as jnp
from jax import lax
from jax.experimental import pallas as pl
from jax.experimental.pallas import tpu as pltpu
from jax.sharding import PartitionSpec as P

MESH = pl.DeviceIdType.MESH
F32, BF16 = jnp.float32, jnp.bfloat16
CAP = 4
LANES = 128
TILE = 512


def dot_t(left, right):
    return lax.dot_general(left, right, (((1,), (1,)), ((), ())), preferred_element_type=F32)


def dot_n(left, right):
    return lax.dot_general(left, right, (((1,), (0,)), ((), ())), preferred_element_type=F32)


def tiles(width):
    return [(start, min(TILE, width - start)) for start in range(0, width, TILE)]


def kernel(
    sizes, tok_ref, ups_ref, ids_ref, rw_ref, gate_ref, up_ref, down_ref,
    dtok_ref, dprob_ref, grad_ref,
    meta, xa, dya, seltr, stage, rows, weights, act, dxs, ret, part,
    fsend, frecv, bsend, brecv, gmine, gsend, gpart, ssend, srecv, gfin, gother,
    send_sem, recv_sem,
):
    nx, ny, nz = sizes
    tok, width = tok_ref.shape
    hid = gate_ref.shape[0]
    half_hid = hid // 2
    experts = ny * nz
    half = nz // 2
    batches = nz // 4
    wide = width + LANES
    mid = width // 2
    block = 4 * CAP
    core, ep, dp = lax.axis_index("rep"), lax.axis_index("ep"), lax.axis_index("dp")
    z, y = ep // ny, lax.rem(ep, ny)

    def at_z(step):
        return (core, lax.rem(z + step + nz, nz) * ny + y, dp)

    def at_y(step):
        return (core, z * ny + lax.rem(y + step, ny), dp)

    def at_x(step):
        return (core, ep, lax.rem(dp + step, nx))

    partner = (1 - core, ep, dp)

    order = [0]
    for step in range(1, half):
        order += [-step, step]
    order.append(half)
    place = {delta: index for index, delta in enumerate(order)}
    place[-half] = place[half]

    started = []

    def send(src, dst, device):
        index = len(started)
        copy = pltpu.make_async_remote_copy(
            src_ref=src, dst_ref=dst, send_sem=send_sem.at[index],
            recv_sem=recv_sem.at[index], device_id=device, device_id_type=MESH,
        )
        copy.start()
        started.append(copy)
        return copy

    barrier = pltpu.get_barrier_semaphore()
    peers = [at_z(1), at_z(-1), partner]
    peers += [at_y(step) for step in range(1, ny)]
    peers += [at_x(1)] if nx == 2 else [at_x(1), at_x(nx - 1)]
    if nx == 4:
        peers.append(at_x(2))
    for peer in peers:
        pl.semaphore_signal(barrier, inc=1, device_id=peer, device_id_type=MESH)
    pl.semaphore_wait(barrier, len(peers))

    xcopy, dcopy, mcopy = {}, {}, {}
    for sign in (-1, 1):
        there = xa.at[place[sign]]
        xcopy[sign] = send(tok_ref, there.at[:, pl.ds(0, width)], at_z(-sign))
    for sign in (-1, 1):
        dcopy[sign] = send(ups_ref, dya.at[place[sign]], at_z(-sign))

    lane = lax.broadcasted_iota(jnp.int32, (tok, LANES), 1)
    routed = jnp.zeros((tok, LANES), F32)
    scale = jnp.zeros((tok, LANES), F32)
    for k in range(4):
        name = ids_ref[:, k:k + 1]
        routed = routed + jnp.where(lane == name, 1.0, 0.0)
        scale = scale + jnp.where(lane == name + 64, rw_ref[:, k:k + 1].astype(F32), 0.0)
    lower = jnp.where(
        lax.broadcasted_iota(jnp.int32, (tok, tok), 1) < lax.broadcasted_iota(jnp.int32, (tok, tok), 0),
        1.0, 0.0,
    ).astype(BF16)
    rank = routed * (dot_n(lower, routed.astype(BF16)) + 1.0)
    own_meta = (rank + scale).astype(BF16)
    meta[...] = own_meta
    for sign in (-1, 1):
        there = xa.at[place[sign]]
        mcopy[sign] = send(meta, there.at[:, pl.ds(width, LANES)], at_z(-sign))

    shard_refs = (gate_ref, up_ref, down_ref)
    mine = pl.ds(pl.multiple_of(core * half_hid, half_hid), half_hid)
    theirs = pl.ds(pl.multiple_of((1 - core) * half_hid, half_hid), half_hid)
    wcopy = {}
    for index, ref in enumerate(shard_refs):
        wcopy[index, nx - 1] = send(ref.at[mine], weights.at[index, nx - 1, 0], at_x(1))
        if nx == 4:
            wcopy[index, 1] = send(ref.at[mine], weights.at[index, 1, 0], at_x(3))
    for index, ref in enumerate(shard_refs):
        weights[index, 0, 0] = ref[mine, :]
        weights[index, 0, 1] = ref[theirs, :]
    xa[0, :, 0:width] = tok_ref[...]
    xa[0, :, width:wide] = own_meta
    dya[0] = ups_ref[...]

    hcopy = []

    def near_weights():
        for index in range(3):
            wcopy[index, nx - 1].wait_recv()
            if nx == 4:
                wcopy[index, 1].wait_recv()
                if index == 1:
                    wcopy[index, 2] = send(weights.at[index, 1, 0], weights.at[index, 2, 0], at_x(3))
                else:
                    wcopy[index, 2] = send(weights.at[index, 3, 0], weights.at[index, 2, 0], at_x(1))
        for index in range(3):
            for rel in ((1, 3) if nx == 4 else (1,)):
                hcopy.append(send(weights.at[index, rel, 0], weights.at[index, rel, 1], partner))

    def far_weights():
        if nx == 4:
            for index in range(3):
                wcopy[index, 2].wait_recv()
                hcopy.append(send(weights.at[index, 2, 0], weights.at[index, 2, 1], partner))

    def all_weights():
        for copy in hcopy:
            copy.wait_recv()

    count = ny * block
    ycopy = {}

    def dispatch(b):
        group = xa[4 * b:4 * b + 4, :, width:wide].reshape(4 * tok, LANES)
        row = lax.broadcasted_iota(jnp.int32, (count, LANES), 0)
        col = lax.broadcasted_iota(jnp.int32, (count, LANES), 1)
        name = z * ny + lax.rem(y + row // block, ny)
        pick = jnp.where(col == name, 1.0, 0.0).astype(BF16)
        pick_w = jnp.where(col == name + 64, 1.0, 0.0).astype(BF16)

        def chosen(value, r, c):
            slot = (lax.rem(r, CAP) + 1).astype(F32)
            return (value == slot) & (c // tok == lax.rem(r // CAP, 4))

        shape = (count, 4 * tok)
        r, c = (lax.broadcasted_iota(jnp.int32, shape, axis) for axis in (0, 1))
        hit = chosen(dot_t(pick, group), r, c)
        sel = jnp.where(hit, 1.0, 0.0).astype(BF16)
        sel_w = jnp.where(hit, dot_t(pick_w, group), 0.0).astype(BF16)
        shape = (4 * tok, count)
        c, r = (lax.broadcasted_iota(jnp.int32, shape, axis) for axis in (0, 1))
        seltr[b] = jnp.where(chosen(dot_t(group, pick), r, c), 1.0, 0.0).astype(BF16)
        for start, size in tiles(width):
            for source, chooser, first in ((xa, sel, 0), (dya, sel_w, block)):
                value = source[4 * b:4 * b + 4, :, start:start + size].reshape(4 * tok, size)
                out = dot_n(chooser, value).astype(BF16).reshape(ny, block, size)
                rows[b, 0, first:first + block, start:start + size] = out[0]
                stage[b, 1:ny, first:first + block, start:start + size] = out[1:ny]
        for step in range(1, ny):
            ycopy[b, step] = send(stage.at[b, step], rows.at[b, ny - step], at_y(step))

    rcopy = {}

    def compute(b):
        for step in range(1, ny):
            ycopy[b, step].wait_recv()
        x_rows = rows[b, :, 0:block, :].reshape(count, width)
        d_rows = rows[b, :, block:2 * block, :].reshape(count, width)
        hidden = nx * hid
        gate_w = weights[0].reshape(hidden, width)
        up_w = weights[1].reshape(hidden, width)
        down_w = weights[2].reshape(hidden, width)
        gate_pre = dot_t(x_rows, gate_w)
        up_pre = dot_t(x_rows, up_w)
        d_act = dot_t(d_rows, down_w)
        sig = jax.nn.sigmoid(gate_pre)
        silu = gate_pre * sig
        act_rows = (silu * up_pre).astype(BF16)
        act[b] = act_rows
        d_gate = (d_act * up_pre * sig * (1.0 + gate_pre * (1.0 - sig))).astype(BF16)
        d_up = (d_act * silu).astype(BF16)
        prob = jnp.sum(act_rows.astype(F32) * d_act, axis=1, keepdims=True)
        here = lax.broadcasted_iota(jnp.int32, (count, LANES), 1) == ep
        extra = jnp.where(here, prob, 0.0).astype(BF16).reshape(ny, block, LANES)
        dxs[b, 1:ny, :, width:wide] = extra[1:ny]
        ret[b, 0, :, width:wide] = extra[0]
        for start, size in tiles(width):
            gate_t = weights[0, :, :, :, start:start + size].reshape(hidden, size)
            up_t = weights[1, :, :, :, start:start + size].reshape(hidden, size)
            out = (dot_n(d_gate, gate_t) + dot_n(d_up, up_t)).astype(BF16).reshape(ny, block, size)
            dxs[b, 1:ny, :, start:start + size] = out[1:ny]
            ret[b, 0, :, start:start + size] = out[0]
        for step in range(1, ny):
            rcopy[b, step] = send(dxs.at[b, step], ret.at[b, ny - step], at_y(step))

    def combine(b):
        for step in range(1, ny):
            rcopy[b, step].wait_recv()
        spread = seltr[b]
        for start, size in tiles(wide):
            value = ret[b, :, :, start:start + size].reshape(count, size)
            out = dot_n(spread, value).reshape(4, tok, size)
            part[4 * b:4 * b + 4, :, start:start + size] = out

    for step in range(1, half + 1):
        if step == 1:
            mcopy[-1].wait_recv()
            mcopy[1].wait_recv()
        for sign, last in ((-1, half), (1, half - 1)):
            if step <= last:
                xcopy[sign * step].wait_recv()
                if step < last:
                    xcopy[sign * (step + 1)] = send(
                        xa.at[place[sign * step]], xa.at[place[sign * (step + 1)]], at_z(-sign)
                    )
        for sign, last in ((-1, half - 1), (1, half)):
            if step <= last:
                dcopy[sign * step].wait_recv()
                if step < last:
                    dcopy[sign * (step + 1)] = send(
                        dya.at[place[sign * step]], dya.at[place[sign * (step + 1)]], at_z(-sign)
                    )
        if step % 2 == 0:
            dispatch(step // 2 - 1)
        if step == max(1, half // 4 + 1):
            near_weights()
        if step == max(1, half // 2):
            far_weights()
        if step == half - 2 and step > 3:
            all_weights()
            compute(0)
        if step == half - 1 and step > 3:
            compute(1)
    if half <= 5:
        all_weights()
    for b in range(2 if half > 5 else 0, batches):
        compute(b)

    act_all = act[...].reshape(batches * count, nx * hid)
    act_t = act_all.T
    for start, size in tiles(width):
        value = rows[:, :, block:2 * block, start:start + size].reshape(batches * count, size)
        out = dot_n(act_t, value).reshape(nx, 2, half_hid, size)
        gmine[:, :, start:start + size] = out[:, 0]
        gsend[:, :, start:start + size] = out[:, 1].astype(BF16)
    gcopy = send(gsend, gpart, partner)

    for b in range(batches):
        combine(b)
        if b == max(0, batches - 2):
            gcopy.wait_recv()
            for rel in range(nx):
                total = gmine[rel] + gpart[rel].astype(F32)
                if rel:
                    ssend[rel] = total.astype(BF16)
                else:
                    gmine[0] = total
            scopy = [send(ssend.at[rel], srecv.at[nx - rel], at_x(rel)) for rel in range(1, nx)]

    cols = (pl.ds(0, mid), pl.ds(mid, wide - mid))
    fcopy, bcopy = {}, {}
    for dist in range(half, 0, -1):
        for col in (0, 1):
            for sign, sends, recvs, copies in ((1, fsend, frecv, fcopy), (-1, bsend, brecv, bcopy)):
                first = half if (col == 0) == (sign == 1) else half - 1
                if dist > first:
                    continue
                value = part[place[sign * dist], :, cols[col]]
                if dist < first:
                    copies[col, dist].wait_recv()
                    value = value + recvs[dist, :, cols[col]].astype(F32)
                sends[dist, :, cols[col]] = value.astype(BF16)
                copies[col, dist - 1] = send(
                    sends.at[dist, :, cols[col]], recvs.at[dist - 1, :, cols[col]], at_z(sign)
                )
        if dist == max(1, half // 2 - 1):
            total = gmine[0]
            for rel in range(1, nx):
                scopy[rel - 1].wait_recv()
            for rel in range(1, nx):
                total = total + srecv[rel].astype(F32)
            gfin[...] = total
            grad_ref[core] = total
            fin = send(gfin, gother, partner)
    fin.wait_recv()
    grad_ref[1 - core] = gother[...]
    for col in (0, 1):
        fcopy[col, 0].wait_recv()
        bcopy[col, 0].wait_recv()
    final = part[0] + frecv[0].astype(F32) + brecv[0].astype(F32)
    dtok_ref[...] = final[:, 0:width].astype(BF16)
    probs = final[:, width:wide]
    slot = lax.broadcasted_iota(jnp.int32, (tok, 4), 1)
    result = jnp.zeros((tok, 4), F32)
    for k in range(4):
        value = jnp.sum(jnp.where(lane == ids_ref[:, k:k + 1], probs, 0.0), axis=1, keepdims=True)
        result = jnp.where(slot == k, value / rw_ref[:, k:k + 1].astype(F32), result)
    dprob_ref[...] = result.astype(BF16)
    for copy in started:
        copy.wait_send()


def local(sizes, tokens, upstream, expert_ids, route_weight, gate_weight, up_weight, down_weight):
    nx, ny, nz = sizes
    tok, width = tokens.shape
    hid = gate_weight.shape[1]
    half_hid, hidden = hid // 2, hid * nx
    half, batches = nz // 2, nz // 4
    wide, block = width + LANES, 4 * CAP
    count = ny * block
    vmem = pl.BlockSpec(memory_space=pltpu.VMEM)
    copies = 512
    d_tokens, d_probs, grad = pl.pallas_call(
        functools.partial(kernel, sizes),
        out_shape=(
            jax.ShapeDtypeStruct((tok, width), BF16),
            jax.ShapeDtypeStruct((tok, 4), BF16),
            jax.ShapeDtypeStruct((2, half_hid, width), F32),
        ),
        in_specs=[vmem] * 7,
        out_specs=(vmem, vmem, vmem),
        scratch_shapes=[
            pltpu.VMEM((tok, LANES), BF16),
            pltpu.VMEM((nz, tok, wide), BF16),
            pltpu.VMEM((nz, tok, width), BF16),
            pltpu.VMEM((batches, 4 * tok, count), BF16),
            pltpu.VMEM((batches, ny, 2 * block, width), BF16),
            pltpu.VMEM((batches, ny, 2 * block, width), BF16),
            pltpu.VMEM((3, nx, 2, half_hid, width), BF16),
            pltpu.VMEM((batches, count, hidden), BF16),
            pltpu.VMEM((batches, ny, block, wide), BF16),
            pltpu.VMEM((batches, ny, block, wide), BF16),
            pltpu.VMEM((nz, tok, wide), F32),
            pltpu.VMEM((half + 1, tok, wide), BF16),
            pltpu.VMEM((half, tok, wide), BF16),
            pltpu.VMEM((half + 1, tok, wide), BF16),
            pltpu.VMEM((half, tok, wide), BF16),
            pltpu.VMEM((nx, half_hid, width), F32),
            pltpu.VMEM((nx, half_hid, width), BF16),
            pltpu.VMEM((nx, half_hid, width), BF16),
            pltpu.VMEM((nx, half_hid, width), BF16),
            pltpu.VMEM((nx, half_hid, width), BF16),
            pltpu.VMEM((half_hid, width), F32),
            pltpu.VMEM((half_hid, width), F32),
            pltpu.SemaphoreType.DMA((160,)),
            pltpu.SemaphoreType.DMA((160,)),
        ],
        compiler_params=pltpu.CompilerParams(
            collective_id=0, has_side_effects=True, vmem_limit_bytes=58 << 20
        ),
    )(
        tokens, upstream, expert_ids, route_weight,
        gate_weight[0], up_weight[0], down_weight[0],
    )
    return d_tokens, d_probs, grad.reshape(1, hid, width)


def build(mesh, ny):
    sizes = (mesh.shape["dp"], ny, mesh.shape["ep"] // ny)
    flat = P(("rep", "ep", "dp"), None)
    split = P("ep", "dp", None)
    return jax.shard_map(
        functools.partial(local, sizes),
        mesh=mesh,
        in_specs=(flat, flat, flat, flat, split, split, split),
        out_specs=(flat, flat, split),
        check_vma=False,
    )


def solution(mesh):
    return build(mesh, 4)
```

time: 323 us -> 125 us (0.39)
  the two profiles are of different devices: /device:TPU:1 before, /device:TPU:32 now
where the time goes in v1:
time: 125 us
  Pallas kernels  117 us (94%)
  local copies, waits for them, and re-layouts  7.03 us (6%)
    pallas_call x1, Pallas kernels, local(): pl.pallas_call(functools.partial(kernel, sizes), out_shape=(jax.ShapeDtyp...  117 us
    unnamed x9, local copies, waits for them, and re-layouts  7.03 us

profile of v1, /device:TPU:32, one launch (start us, length us, event | category | flops | bytes accessed | tf_op | source)
XLA Modules:
  0.0 124.8 jit_solution(1128523021311733419)
XLA Ops:
  0.6 0.0 copy-start.1
  0.6 0.7 copy-done.1
  1.3 0.0 copy-start
  1.3 0.7 copy.11.rw_ref
  2.0 0.0 copy-done
  2.0 0.7 copy.10.ids_ref
  2.7 117.1 %shard_map.94 = (bf16[32,2048]{1,0:T(8,128)(2,1)}, bf16[32,4]{1,0:T(8,128)(2,1)}, f32[2,48,2048]{2,1,0:T(8,128)}) custom-call(bf16[32,2048]{1,0:T(8,128)(2,1)} %tok_ref.1, bf16[32,2048]{1,0:T(8,128)(2,1)} %ups_ref.1, s32[32,4]{1,0:T(8,128)} %copy.10.ids_ref, bf16[32,4]{1,0:T(8,128)(2,1)} %copy.11.rw_ref, bf16[96,2048]{1,0:T(8,128)(2,1)} %bitcast.5, ...), custom_call_target="tpu_custom_call" | custom-call | tf_op jit(solution)/shard_map/pallas_call | solution.py:337
  119.8 1.3 %copy.12 = bf16[32,4]{0,1:T(4,128)(2,1)} copy(bf16[32,4]{1,0:T(8,128)(2,1)} %get-tuple-element.10) | data formatting | bytes 512
  121.1 1.6 %copy.15 = bf16[32,2048]{1,0:T(8,128)(2,1)} copy(bf16[32,2048]{1,0:T(8,128)(2,1)} %get-tuple-element.15) | data formatting | bytes 262144
  122.7 2.1 %copy.16 = f32[1,96,2048]{2,1,0:T(8,128)} copy(f32[1,96,2048]{2,1,0:T(8,128)} %bitcast.4) | data formatting | bytes 1572864
Async XLA Ops:
  0.6 0.7 copy-start.1
  1.3 0.7 copy-start

commit v2 on v1

v2 whole, which is shorter than its diff:
```python
import functools

import jax
import jax.numpy as jnp
from jax import lax
from jax.experimental import pallas as pl
from jax.experimental.pallas import tpu as pltpu
from jax.sharding import PartitionSpec as P

MESH = pl.DeviceIdType.MESH
F32, BF16 = jnp.float32, jnp.bfloat16
CAP = 4
LANES = 128
TILE = 512


def dot_t(left, right):
    return lax.dot_general(left, right, (((1,), (1,)), ((), ())), preferred_element_type=F32)


def dot_n(left, right):
    return lax.dot_general(left, right, (((1,), (0,)), ((), ())), preferred_element_type=F32)


def tiles(width):
    return [(start, min(TILE, width - start)) for start in range(0, width, TILE)]


def kernel(
    sizes, tok_ref, ups_ref, ids_ref, rw_ref, gate_ref, up_ref, down_ref,
    total_ref, grad_ref,
    meta, xa, dya, seltr, stage, rows, weights, act, dgate, dup, dxs, ret, part,
    fsend, frecv, bsend, brecv, gacc, gsend, gpart, ssend, srecv, gfin, gother,
    send_sem, recv_sem, local_sem,
):
    nx, ny, nz = sizes
    tok, width = tok_ref.shape
    hid = gate_ref.shape[0]
    half_hid = hid // 2
    hidden = nx * hid
    half = nz // 2
    batches = nz // 4
    pairs = nz // 2
    wide = width + LANES
    mid = width // 2
    core, ep, dp = lax.axis_index("rep"), lax.axis_index("ep"), lax.axis_index("dp")
    z, y = ep // ny, lax.rem(ep, ny)

    def at_z(step):
        return (core, lax.rem(z + step + nz, nz) * ny + y, dp)

    def at_y(step):
        return (core, z * ny + lax.rem(y + step, ny), dp)

    def at_x(step):
        return (core, ep, lax.rem(dp + step, nx))

    partner = (1 - core, ep, dp)

    order = [0]
    for step in range(1, half):
        order += [-step, step]
    order.append(half)
    place = {delta: index for index, delta in enumerate(order)}
    place[-half] = place[half]

    started = []

    def send(src, dst, device):
        index = len(started)
        copy = pltpu.make_async_remote_copy(
            src_ref=src, dst_ref=dst, send_sem=send_sem.at[index],
            recv_sem=recv_sem.at[index], device_id=device, device_id_type=MESH,
        )
        copy.start()
        started.append(copy)
        return copy

    shard_refs = (gate_ref, up_ref, down_ref)
    mine = pl.ds(pl.multiple_of(core * half_hid, half_hid), half_hid)
    theirs = pl.ds(pl.multiple_of((1 - core) * half_hid, half_hid), half_hid)
    loads = [(tok_ref, xa.at[0, :, pl.ds(0, width)]), (ups_ref, dya.at[0])]
    for index, ref in enumerate(shard_refs):
        loads.append((ref.at[mine], weights.at[index, 0, 0]))
        loads.append((ref.at[theirs], weights.at[index, 0, 1]))
    loads = [
        pltpu.make_async_copy(src, dst, local_sem.at[index])
        for index, (src, dst) in enumerate(loads)
    ]
    for copy in loads:
        copy.start()

    barrier = pltpu.get_barrier_semaphore()
    peers = [at_z(1), at_z(-1), partner]
    peers += [at_y(step) for step in range(1, ny)]
    peers += [at_x(step) for step in range(1, nx)]
    for peer in peers:
        pl.semaphore_signal(barrier, inc=1, device_id=peer, device_id_type=MESH)
    pl.semaphore_wait(barrier, len(peers))

    xcopy, dcopy, mcopy = {}, {}, {}
    for sign in (-1, 1):
        xcopy[sign] = send(tok_ref, xa.at[place[sign], :, pl.ds(0, width)], at_z(-sign))

    name = lax.broadcasted_iota(jnp.int32, (LANES, tok), 0)
    scales = rw_ref[...].astype(F32)
    routed = jnp.zeros((LANES, tok), F32)
    scale = jnp.zeros((LANES, tok), F32)
    for k in range(4):
        chosen_name = ids_ref[k:k + 1, :]
        routed = routed + jnp.where(name == chosen_name, 1.0, 0.0)
        scale = scale + jnp.where(name == chosen_name + 64, scales[k:k + 1, :], 0.0)
    first = lax.broadcasted_iota(jnp.int32, (tok, tok), 0)
    second = lax.broadcasted_iota(jnp.int32, (tok, tok), 1)
    upper = jnp.where(first < second, 1.0, 0.0).astype(BF16)
    same = jnp.where(first == second, 1.0, 0.0).astype(BF16)
    rank = routed * (dot_n(routed.astype(BF16), upper) + 1.0)
    own_meta = dot_t(same, (rank + scale).astype(BF16)).astype(BF16)
    meta[...] = own_meta
    for sign in (-1, 1):
        mcopy[sign] = send(meta, xa.at[place[sign], :, pl.ds(width, LANES)], at_z(-sign))
    for sign in (-1, 1):
        dcopy[sign] = send(ups_ref, dya.at[place[sign]], at_z(-sign))
    xa[0, :, width:wide] = own_meta

    wcopy = {}
    for index, ref in enumerate(shard_refs):
        wcopy[index, nx - 1] = send(ref.at[mine], weights.at[index, nx - 1, 0], at_x(1))
        if nx == 4:
            wcopy[index, 1] = send(ref.at[mine], weights.at[index, 1, 0], at_x(3))
    for copy in loads:
        copy.wait()

    hcopy = []

    def near_weights():
        for index in range(3):
            wcopy[index, nx - 1].wait_recv()
            if nx == 4:
                wcopy[index, 1].wait_recv()
                if index == 1:
                    wcopy[index, 2] = send(weights.at[index, 1, 0], weights.at[index, 2, 0], at_x(3))
                else:
                    wcopy[index, 2] = send(weights.at[index, 3, 0], weights.at[index, 2, 0], at_x(1))
        for index in range(3):
            for rel in ((1, 3) if nx == 4 else (1,)):
                hcopy.append(send(weights.at[index, rel, 0], weights.at[index, rel, 1], partner))

    def far_weights():
        if nx == 4:
            for index in range(3):
                wcopy[index, 2].wait_recv()
                hcopy.append(send(weights.at[index, 2, 0], weights.at[index, 2, 1], partner))

    def all_weights():
        for copy in hcopy:
            copy.wait_recv()

    ycopy = {}
    block = 2 * CAP
    count = ny * block

    def chosen(value, r, c, sources):
        slot = (lax.rem(r, CAP) + 1).astype(F32)
        return (value == slot) & (c // tok == lax.rem(r // CAP, sources))

    def picks(size, row_block):
        row = lax.broadcasted_iota(jnp.int32, (size, LANES), 0)
        col = lax.broadcasted_iota(jnp.int32, (size, LANES), 1)
        expert = z * ny + lax.rem(y + row // row_block, ny)
        pick = jnp.where(col == expert, 1.0, 0.0).astype(BF16)
        pick_w = jnp.where(col == expert + 64, 1.0, 0.0).astype(BF16)
        return pick, pick_w

    def dispatch(p):
        group = xa[2 * p:2 * p + 2, :, width:wide].reshape(2 * tok, LANES)
        pick, pick_w = picks(count, block)
        shape = (count, 2 * tok)
        r, c = (lax.broadcasted_iota(jnp.int32, shape, axis) for axis in (0, 1))
        hit = chosen(dot_t(pick, group), r, c, 2)
        sel = jnp.where(hit, 1.0, 0.0).astype(BF16)
        sel_w = jnp.where(hit, dot_t(pick_w, group), 0.0).astype(BF16)
        for start, size in tiles(width):
            parts = []
            for source, chooser in ((xa, sel), (dya, sel_w)):
                value = source[2 * p:2 * p + 2, :, start:start + size].reshape(2 * tok, size)
                parts.append(dot_n(chooser, value).reshape(ny, block, size))
            out = jnp.concatenate(parts, axis=1).astype(BF16)
            rows[p, 0, :, start:start + size] = out[0]
            stage[p, 1:ny, :, start:start + size] = out[1:ny]
        for step in range(1, ny):
            ycopy[p, step] = send(stage.at[p, step], rows.at[p, ny - step], at_y(step))

    rcopy = {}
    cols = (pl.ds(0, mid), pl.ds(mid, wide - mid))

    def split(value):
        value = value.reshape(2 * ny, 2, block, hidden)
        return value[:, 0], value[:, 1]

    def forward(b):
        for p in (2 * b, 2 * b + 1):
            for step in range(1, ny):
                ycopy[p, step].wait_recv()
        both = rows[2 * b:2 * b + 2].reshape(4 * count, width)
        gate_pre, _ = split(dot_t(both, weights[0].reshape(hidden, width)))
        up_pre, _ = split(dot_t(both, weights[1].reshape(hidden, width)))
        _, d_act = split(dot_t(both, weights[2].reshape(hidden, width)))
        sig = jax.nn.sigmoid(gate_pre)
        silu = gate_pre * sig
        act_rows = (silu * up_pre).astype(BF16).astype(F32)
        act[b] = jnp.concatenate([jnp.zeros_like(act_rows), act_rows], axis=1).reshape(4 * count, hidden).astype(BF16)
        d_gate = d_act * up_pre * sig * (1.0 + gate_pre * (1.0 - sig))
        dgate[...] = d_gate.reshape(2 * count, hidden).astype(BF16)
        dup[...] = (d_act * silu).reshape(2 * count, hidden).astype(BF16)
        prob = jnp.sum(act_rows * d_act, axis=2, keepdims=True)
        here = lax.broadcasted_iota(jnp.int32, (2 * ny, block, LANES), 2) == ep
        give(b, width, LANES, jnp.where(here, prob, 0.0))

    def give(b, start, size, value):
        value = value.reshape(2, ny, block, size)
        value = jnp.concatenate([value[0], value[1]], axis=1).astype(BF16)
        dxs[b, 1:ny, :, start:start + size] = value[1:ny]
        ret[b, 0, :, start:start + size] = value[0]

    def backward(b):
        d_gate, d_up = dgate[...], dup[...]
        done = 0
        for start, size in tiles(width):
            gate_t = weights[0, :, :, :, start:start + size].reshape(hidden, size)
            up_t = weights[1, :, :, :, start:start + size].reshape(hidden, size)
            give(b, start, size, dot_n(d_gate, gate_t) + dot_n(d_up, up_t))
            if done == 0 and start + size >= mid or start + size == width:
                for step in range(1, ny):
                    rcopy[b, done, step] = send(
                        dxs.at[b, step, :, cols[done]], ret.at[b, ny - step, :, cols[done]], at_y(step)
                    )
                done += 1

    def spread(b):
        group = xa[4 * b:4 * b + 4, :, width:wide].reshape(4 * tok, LANES)
        pick, _ = picks(2 * count, 2 * block)
        shape = (4 * tok, 2 * count)
        c, r = (lax.broadcasted_iota(jnp.int32, shape, axis) for axis in (0, 1))
        seltr[b] = jnp.where(chosen(dot_t(group, pick), r, c, 4), 1.0, 0.0).astype(BF16)

    def combine(b, col):
        for step in range(1, ny):
            rcopy[b, col, step].wait_recv()
        low, high = ((0, mid), (mid, wide))[col]
        for start, size in tiles(high - low):
            start += low
            value = ret[b, :, :, start:start + size].reshape(2 * count, size)
            out = dot_n(seltr[b], value).reshape(4, tok, size)
            part[4 * b:4 * b + 4, :, start:start + size] = out

    def grads(b):
        act_t = act[b].T
        for start, size in tiles(width):
            value = rows[2 * b:2 * b + 2, :, :, start:start + size].reshape(4 * count, size)
            out = dot_n(act_t, value).reshape(nx, 2, half_hid, size)
            if b:
                out = out + gacc[:, :, :, start:start + size]
            gacc[:, :, :, start:start + size] = out
            if b == batches - 1:
                gsend[:, :, start:start + size] = out[:, 1].astype(BF16)

    if half == 8:
        table = {
            4: [near_weights], 8: [far_weights], 9: [all_weights],
            10: [lambda: forward(0)], 11: [lambda: backward(0)],
            12: [lambda: forward(1)], 13: [lambda: backward(1)],
            14: [lambda: grads(0)], 15: [lambda: grads(1)],
            17: [lambda: forward(2), lambda: backward(2), lambda: grads(2)],
        }
    else:
        table = {2 * half + 1: [near_weights, far_weights, all_weights]}
        for b in range(batches - 1):
            table[2 * half + 1] += [
                functools.partial(forward, b), functools.partial(backward, b), functools.partial(grads, b)
            ]

    for step in range(1, half + 1):
        if step == 1:
            mcopy[-1].wait_recv()
            mcopy[1].wait_recv()
        for moving, copies, ends, slot in (
            (xa, xcopy, (half, half - 1), 2 * step), (dya, dcopy, (half - 1, half), 2 * step + 1),
        ):
            for sign, last in zip((-1, 1), ends):
                if step <= last:
                    copies[sign * step].wait_recv()
                    if step < last:
                        copies[sign * (step + 1)] = send(
                            moving.at[place[sign * step]], moving.at[place[sign * (step + 1)]], at_z(-sign)
                        )
            if slot == 2 * step + 1:
                dispatch(step - 1)
            for task in table.get(slot, ()):
                task()

    last = batches - 1
    forward(last)
    backward(last)
    grads(last)
    gcopy = send(gsend, gpart, partner)
    for b in range(batches):
        spread(b)
    for b in range(batches - 1):
        for col in (0, 1):
            combine(b, col)

    def pair_sum():
        gcopy.wait_recv()
        for rel in range(nx):
            total = gacc[rel, 0] + gpart[rel].astype(F32)
            if rel:
                ssend[rel] = total.astype(BF16)
            else:
                gacc[0, 0] = total
        return [send(ssend.at[rel], srecv.at[nx - rel], at_x(rel)) for rel in range(1, nx)]

    fcopy, bcopy = {}, {}
    for dist in range(half, 0, -1):
        for col in (0, 1):
            if dist == half:
                combine(last, col)
            for sign, sends, recvs, copies in ((1, fsend, frecv, fcopy), (-1, bsend, brecv, bcopy)):
                first = half if (col == 0) == (sign == 1) else half - 1
                if dist > first:
                    continue
                value = part[place[sign * dist], :, cols[col]]
                if dist < first:
                    copies[col, dist].wait_recv()
                    value = value + recvs[dist, :, cols[col]].astype(F32)
                sends[dist, :, cols[col]] = value.astype(BF16)
                copies[col, dist - 1] = send(
                    sends.at[dist, :, cols[col]], recvs.at[dist - 1, :, cols[col]], at_z(sign)
                )
        if dist == half:
            scopy = pair_sum()
        if dist == max(1, half // 4):
            total = gacc[0, 0]
            for rel in range(1, nx):
                scopy[rel - 1].wait_recv()
            for rel in range(1, nx):
                total = total + srecv[rel].astype(F32)
            gfin[...] = total
            grad_ref[core] = total
            fin = send(gfin, gother, partner)
    fin.wait_recv()
    grad_ref[1 - core] = gother[...]
    for col in (0, 1):
        fcopy[col, 0].wait_recv()
        bcopy[col, 0].wait_recv()
    total_ref[...] = part[0] + frecv[0].astype(F32) + brecv[0].astype(F32)
    for copy in started:
        copy.wait_send()


def finish(total_any, halves_ref, ids_ref, rw_ref, dtok_ref, dprob_ref, grad_ref, total_ref, sem):
    tok, width = dtok_ref.shape
    grad_copy = pltpu.make_async_copy(halves_ref, grad_ref, sem.at[0])
    total_copy = pltpu.make_async_copy(total_any, total_ref, sem.at[1])
    total_copy.start()
    grad_copy.start()
    total_copy.wait()
    dtok_ref[...] = total_ref[:, 0:width].astype(BF16)
    probs = total_ref[:, width:width + LANES].astype(BF16)
    name = lax.broadcasted_iota(jnp.int32, (LANES, LANES), 0)
    other = lax.broadcasted_iota(jnp.int32, (LANES, LANES), 1)
    same = jnp.where(name == other, 1.0, 0.0).astype(BF16)
    probs = dot_t(same, probs)
    name = lax.broadcasted_iota(jnp.int32, (LANES, tok), 0)
    slot = lax.broadcasted_iota(jnp.int32, (4, tok), 0)
    values = jnp.zeros((4, tok), F32)
    for k in range(4):
        value = jnp.sum(jnp.where(name == ids_ref[k:k + 1, :], probs, 0.0), axis=0, keepdims=True)
        values = jnp.where(slot == k, value, values)
    dprob_ref[...] = (values / rw_ref[...].astype(F32)).astype(BF16)
    grad_copy.wait()


def local(sizes, tokens, upstream, expert_ids, route_weight, gate_weight, up_weight, down_weight):
    nx, ny, nz = sizes
    tok, width = tokens.shape
    hid = gate_weight.shape[1]
    half_hid, hidden = hid // 2, hid * nx
    half, batches = nz // 2, nz // 4
    wide, block = width + LANES, 4 * CAP
    count = ny * block
    vmem = pl.BlockSpec(memory_space=pltpu.VMEM)
    hbm = pl.BlockSpec(memory_space=pltpu.HBM)
    anywhere = pl.BlockSpec(memory_space=pl.ANY)
    ids, scales = expert_ids.T, route_weight.T

    def stay(value):
        return pltpu.with_memory_space_constraint(value, pltpu.HBM)

    total, halves = pl.pallas_call(
        functools.partial(kernel, sizes),
        out_shape=(
            jax.ShapeDtypeStruct((tok, wide), F32),
            jax.ShapeDtypeStruct((2, half_hid, width), F32),
        ),
        in_specs=[hbm, hbm, vmem, vmem, hbm, hbm, hbm],
        out_specs=(vmem, vmem),
        scratch_shapes=[
            pltpu.VMEM((tok, LANES), BF16),
            pltpu.VMEM((nz, tok, wide), BF16),
            pltpu.VMEM((nz, tok, width), BF16),
            pltpu.VMEM((batches, 4 * tok, count), BF16),
            pltpu.VMEM((nz // 2, ny, block, width), BF16),
            pltpu.VMEM((nz // 2, ny, block, width), BF16),
            pltpu.VMEM((3, nx, 2, half_hid, width), BF16),
            pltpu.VMEM((batches, 2 * count, hidden), BF16),
            pltpu.VMEM((count, hidden), BF16),
            pltpu.VMEM((count, hidden), BF16),
            pltpu.VMEM((batches, ny, block, wide), BF16),
            pltpu.VMEM((batches, ny, block, wide), BF16),
            pltpu.VMEM((nz, tok, wide), F32),
            pltpu.VMEM((half + 1, tok, wide), BF16),
            pltpu.VMEM((half, tok, wide), BF16),
            pltpu.VMEM((half + 1, tok, wide), BF16),
            pltpu.VMEM((half, tok, wide), BF16),
            pltpu.VMEM((nx, 2, half_hid, width), F32),
            pltpu.VMEM((nx, half_hid, width), BF16),
            pltpu.VMEM((nx, half_hid, width), BF16),
            pltpu.VMEM((nx, half_hid, width), BF16),
            pltpu.VMEM((nx, half_hid, width), BF16),
            pltpu.VMEM((half_hid, width), F32),
            pltpu.VMEM((half_hid, width), F32),
            pltpu.SemaphoreType.DMA((192,)),
            pltpu.SemaphoreType.DMA((192,)),
            pltpu.SemaphoreType.DMA((8,)),
        ],
        compiler_params=pltpu.CompilerParams(
            collective_id=0, has_side_effects=True, vmem_limit_bytes=48 << 20
        ),
    )(
        stay(tokens), stay(upstream), ids, scales,
        stay(gate_weight[0]), stay(up_weight[0]), stay(down_weight[0]),
    )
    d_tokens, d_probs, grad = pl.pallas_call(
        finish,
        out_shape=(
            jax.ShapeDtypeStruct((tok, width), BF16),
            jax.ShapeDtypeStruct((4, tok), BF16),
            jax.ShapeDtypeStruct((2, half_hid, width), F32),
        ),
        in_specs=[anywhere, anywhere, vmem, vmem],
        out_specs=(vmem, vmem, anywhere),
        scratch_shapes=[pltpu.VMEM((tok, wide), F32), pltpu.SemaphoreType.DMA((2,))],
        compiler_params=pltpu.CompilerParams(vmem_limit_bytes=8 << 20),
    )(total, halves, ids, scales)
    return d_tokens, d_probs.T, grad.reshape(1, hid, width)


def build(mesh, ny):
    sizes = (mesh.shape["dp"], ny, mesh.shape["ep"] // ny)
    flat = P(("rep", "ep", "dp"), None)
    split = P("ep", "dp", None)
    return jax.shard_map(
        functools.partial(local, sizes),
        mesh=mesh,
        in_specs=(flat, flat, flat, flat, split, split, split),
        out_specs=(flat, flat, split),
        check_vma=False,
    )


def solution(mesh):
    return build(mesh, 4)
```

time: 125 us -> 112 us (0.90)
  the two profiles are of different devices: /device:TPU:32 before, /device:TPU:2 now
where the time goes in v2:
time: 112 us
  Pallas kernels  110 us (98%)
    pallas_call x1, Pallas kernels, local(): pl.pallas_call(functools.partial(kernel, sizes), out_shape=(jax.ShapeDtyp...  109 us

profile of v2, /device:TPU:2, one launch (start us, length us, event | category | flops | bytes accessed | tf_op | source)
XLA Modules:
  0.0 111.8 jit_solution(1555421040463472614)
XLA Ops:
  0.6 0.0 copy-start
  0.6 0.0 copy-start.1
  0.7 0.7 copy-done
  1.3 0.0 copy-done.1
  1.3 108.8 %shard_map.94 = (f32[32,2176]{1,0:T(8,128)S(1)}, f32[2,48,2048]{2,1,0:T(8,128)S(1)}) custom-call(bf16[32,2048]{1,0:T(8,128)(2,1)} %tok_ref.1, bf16[32,2048]{1,0:T(8,128)(2,1)} %ups_ref.1, s32[4,32]{1,0:T(4,128)S(1)} %bitcast.7, bf16[4,32]{1,0:T(4,128)(2,1)S(1)} %bitcast.9, bf16[96,2048]{1,0:T(8,128)(2,1)} %bitcast.11, bf16[96,2048]{1,0:T(8,128)(2,1)} %bitcast.12, ...), custom_call_target="tpu_custom_call" | custom-call | tf_op jit(solution)/shard_map/pallas_call | solution.py:400
  110.2 1.6 %shard_map.95 = (bf16[32,2048]{1,0:T(8,128)(2,1)}, bf16[4,32]{1,0:T(4,128)(2,1)}, f32[2,48,2048]{2,1,0:T(8,128)}) custom-call(f32[32,2176]{1,0:T(8,128)S(1)} %get-tuple-element.8.total_any, f32[2,48,2048]{2,1,0:T(8,128)S(1)} %get-tuple-element.9.halves_ref, s32[4,32]{1,0:T(4,128)S(1)} %bitcast.8, bf16[4,32]{1,0:T(4,128)(2,1)S(1)} %bitcast.10), custom_call_target="tpu_custom_call" | custom-call | tf_op jit(solution)/shard_map/pallas_call | solution.py:444
Async XLA Ops:
  0.6 0.7 copy-start
  0.6 0.7 copy-start.1

commit v3 on v2

--- a/solution.py
+++ b/solution.py
@@ -31,7 +31,7 @@
     total_ref, grad_ref,
     meta, xa, dya, seltr, stage, rows, weights, act, dgate, dup, dxs, ret, part,
     fsend, frecv, bsend, brecv, gacc, gsend, gpart, ssend, srecv, gfin, gother,
-    send_sem, recv_sem, local_sem,
+    ids_own, rw_own, send_sem, recv_sem, local_sem,
 ):
     nx, ny, nz = sizes
     tok, width = tok_ref.shape
@@ -42,7 +42,6 @@
     batches = nz // 4
     pairs = nz // 2
     wide = width + LANES
-    mid = width // 2
     core, ep, dp = lax.axis_index("rep"), lax.axis_index("ep"), lax.axis_index("dp")
     z, y = ep // ny, lax.rem(ep, ny)
 
@@ -79,7 +78,7 @@
     shard_refs = (gate_ref, up_ref, down_ref)
     mine = pl.ds(pl.multiple_of(core * half_hid, half_hid), half_hid)
     theirs = pl.ds(pl.multiple_of((1 - core) * half_hid, half_hid), half_hid)
-    loads = [(tok_ref, xa.at[0, :, pl.ds(0, width)]), (ups_ref, dya.at[0])]
+    loads = [(ids_ref, ids_own), (rw_ref, rw_own), (tok_ref, xa.at[0, :, pl.ds(0, width)]), (ups_ref, dya.at[0])]
     for index, ref in enumerate(shard_refs):
         loads.append((ref.at[mine], weights.at[index, 0, 0]))
         loads.append((ref.at[theirs], weights.at[index, 0, 1]))
@@ -96,18 +95,30 @@
     peers += [at_x(step) for step in range(1, nx)]
     for peer in peers:
         pl.semaphore_signal(barrier, inc=1, device_id=peer, device_id_type=MESH)
+    loads[0].wait()
+    loads[1].wait()
     pl.semaphore_wait(barrier, len(peers))
 
     xcopy, dcopy, mcopy = {}, {}, {}
-    for sign in (-1, 1):
+
+    def first_x(sign):
         xcopy[sign] = send(tok_ref, xa.at[place[sign], :, pl.ds(0, width)], at_z(-sign))
 
+    def first_d(sign):
+        dcopy[sign] = send(ups_ref, dya.at[place[sign]], at_z(-sign))
+
+    def first_m(sign):
+        mcopy[sign] = send(meta, xa.at[place[sign], :, pl.ds(width, LANES)], at_z(-sign))
+
+    first_x(-1)
+    first_d(1)
+
     name = lax.broadcasted_iota(jnp.int32, (LANES, tok), 0)
-    scales = rw_ref[...].astype(F32)
+    scales = rw_own[...].astype(F32)
     routed = jnp.zeros((LANES, tok), F32)
     scale = jnp.zeros((LANES, tok), F32)
     for k in range(4):
-        chosen_name = ids_ref[k:k + 1, :]
+        chosen_name = ids_own[k:k + 1, :]
         routed = routed + jnp.where(name == chosen_name, 1.0, 0.0)
         scale = scale + jnp.where(name == chosen_name + 64, scales[k:k + 1, :], 0.0)
     first = lax.broadcasted_iota(jnp.int32, (tok, tok), 0)
@@ -117,10 +128,10 @@
     rank = routed * (dot_n(routed.astype(BF16), upper) + 1.0)
     own_meta = dot_t(same, (rank + scale).astype(BF16)).astype(BF16)
     meta[...] = own_meta
-    for sign in (-1, 1):
-        mcopy[sign] = send(meta, xa.at[place[sign], :, pl.ds(width, LANES)], at_z(-sign))
-    for sign in (-1, 1):
-        dcopy[sign] = send(ups_ref, dya.at[place[sign]], at_z(-sign))
+    first_m(-1)
+    first_x(1)
+    first_m(1)
+    first_d(-1)
     xa[0, :, width:wide] = own_meta
 
     wcopy = {}
@@ -128,7 +139,7 @@
         wcopy[index, nx - 1] = send(ref.at[mine], weights.at[index, nx - 1, 0], at_x(1))
         if nx == 4:
             wcopy[index, 1] = send(ref.at[mine], weights.at[index, 1, 0], at_x(3))
-    for copy in loads:
+    for copy in loads[2:]:
         copy.wait()
 
     hcopy = []
@@ -192,7 +203,8 @@
             ycopy[p, step] = send(stage.at[p, step], rows.at[p, ny - step], at_y(step))
 
     rcopy = {}
-    cols = (pl.ds(0, mid), pl.ds(mid, wide - mid))
+    edges = [(width // 4 * c, width // 4 if c < 3 else wide - width // 4 * 3) for c in range(4)]
+    cols = [pl.ds(start, size) for start, size in edges]
 
     def split(value):
         value = value.reshape(2 * ny, 2, block, hidden)
@@ -225,17 +237,19 @@
 
     def backward(b):
         d_gate, d_up = dgate[...], dup[...]
-        done = 0
-        for start, size in tiles(width):
+        for col in range(4):
+            start, size = width // 4 * col, width // 4
             gate_t = weights[0, :, :, :, start:start + size].reshape(hidden, size)
             up_t = weights[1, :, :, :, start:start + size].reshape(hidden, size)
             give(b, start, size, dot_n(d_gate, gate_t) + dot_n(d_up, up_t))
-            if done == 0 and start + size >= mid or start + size == width:
+            if b == batches - 1:
                 for step in range(1, ny):
-                    rcopy[b, done, step] = send(
-                        dxs.at[b, step, :, cols[done]], ret.at[b, ny - step, :, cols[done]], at_y(step)
+                    rcopy[b, col, step] = send(
+                        dxs.at[b, step, :, cols[col]], ret.at[b, ny - step, :, cols[col]], at_y(step)
                     )
-                done += 1
+        if b < batches - 1:
+            for step in range(1, ny):
+                rcopy[b, 0, step] = send(dxs.at[b, step], ret.at[b, ny - step], at_y(step))
 
     def spread(b):
         group = xa[4 * b:4 * b + 4, :, width:wide].reshape(4 * tok, LANES)
@@ -245,14 +259,12 @@
         seltr[b] = jnp.where(chosen(dot_t(group, pick), r, c, 4), 1.0, 0.0).astype(BF16)
 
     def combine(b, col):
-        for step in range(1, ny):
-            rcopy[b, col, step].wait_recv()
-        low, high = ((0, mid), (mid, wide))[col]
-        for start, size in tiles(high - low):
-            start += low
-            value = ret[b, :, :, start:start + size].reshape(2 * count, size)
-            out = dot_n(seltr[b], value).reshape(4, tok, size)
-            part[4 * b:4 * b + 4, :, start:start + size] = out
+        if (b, col, ny - 1) in rcopy:
+            for step in range(1, ny):
+                rcopy[b, col, step].wait_recv()
+        start, size = edges[col]
+        value = ret[b, :, :, start:start + size].reshape(2 * count, size)
+        part[4 * b:4 * b + 4, :, start:start + size] = dot_n(seltr[b], value).reshape(4, tok, size)
 
     def grads(b):
         act_t = act[b].T
@@ -281,15 +293,15 @@
             ]
 
     for step in range(1, half + 1):
-        if step == 1:
-            mcopy[-1].wait_recv()
-            mcopy[1].wait_recv()
-        for moving, copies, ends, slot in (
-            (xa, xcopy, (half, half - 1), 2 * step), (dya, dcopy, (half - 1, half), 2 * step + 1),
+        for slot, routes in (
+            (2 * step, ((xa, xcopy, -1, half), (dya, dcopy, 1, half))),
+            (2 * step + 1, ((dya, dcopy, -1, half - 1), (xa, xcopy, 1, half - 1))),
         ):
-            for sign, last in zip((-1, 1), ends):
+            for moving, copies, sign, last in routes:
                 if step <= last:
                     copies[sign * step].wait_recv()
+                    if step == 1 and moving is xa:
+                        mcopy[sign].wait_recv()
                     if step < last:
                         copies[sign * (step + 1)] = send(
                             moving.at[place[sign * step]], moving.at[place[sign * (step + 1)]], at_z(-sign)
@@ -307,7 +319,7 @@
     for b in range(batches):
         spread(b)
     for b in range(batches - 1):
-        for col in (0, 1):
+        for col in range(4):
             combine(b, col)
 
     def pair_sum():
@@ -320,26 +332,30 @@
                 gacc[0, 0] = total
         return [send(ssend.at[rel], srecv.at[nx - rel], at_x(rel)) for rel in range(1, nx)]
 
-    fcopy, bcopy = {}, {}
-    for dist in range(half, 0, -1):
-        for col in (0, 1):
-            if dist == half:
+    chain = {}
+
+    def relay(col, sign, dist):
+        sends, recvs = (fsend, frecv) if sign == 1 else (bsend, brecv)
+        value = part[place[sign * dist], :, cols[col]]
+        if (col, sign, dist) in chain:
+            chain[col, sign, dist].wait_recv()
+            value = value + recvs[dist, :, cols[col]].astype(F32)
+        sends[dist, :, cols[col]] = value.astype(BF16)
+        chain[col, sign, dist - 1] = send(
+            sends.at[dist, :, cols[col]], recvs.at[dist - 1, :, cols[col]], at_z(sign)
+        )
+
+    for turn in range(half):
+        for col in range(4):
+            if turn == 0:
                 combine(last, col)
-            for sign, sends, recvs, copies in ((1, fsend, frecv, fcopy), (-1, bsend, brecv, bcopy)):
-                first = half if (col == 0) == (sign == 1) else half - 1
-                if dist > first:
-                    continue
-                value = part[place[sign * dist], :, cols[col]]
-                if dist < first:
-                    copies[col, dist].wait_recv()
-                    value = value + recvs[dist, :, cols[col]].astype(F32)
-                sends[dist, :, cols[col]] = value.astype(BF16)
-                copies[col, dist - 1] = send(
-                    sends.at[dist, :, cols[col]], recvs.at[dist - 1, :, cols[col]], at_z(sign)
-                )
-        if dist == half:
+            long = 1 if col % 2 == 0 else -1
+            relay(col, long, half - turn)
+            if turn < half - 1:
+                relay(col, -long, half - 1 - turn)
+        if turn == 0:
             scopy = pair_sum()
-        if dist == max(1, half // 4):
+        if turn == max(0, half - 3):
             total = gacc[0, 0]
             for rel in range(1, nx):
                 scopy[rel - 1].wait_recv()
@@ -350,20 +366,27 @@
             fin = send(gfin, gother, partner)
     fin.wait_recv()
     grad_ref[1 - core] = gother[...]
-    for col in (0, 1):
-        fcopy[col, 0].wait_recv()
-        bcopy[col, 0].wait_recv()
-    total_ref[...] = part[0] + frecv[0].astype(F32) + brecv[0].astype(F32)
+    for col in range(4):
+        chain[col, 1, 0].wait_recv()
+        chain[col, -1, 0].wait_recv()
+        start, size = edges[col]
+        total_ref[:, start:start + size] = (
+            part[0, :, start:start + size]
+            + frecv[0, :, start:start + size].astype(F32)
+            + brecv[0, :, start:start + size].astype(F32)
+        )
     for copy in started:
         copy.wait_send()
 
 
-def finish(total_any, halves_ref, ids_ref, rw_ref, dtok_ref, dprob_ref, grad_ref, total_ref, sem):
+def finish(total_any, halves_ref, ids_any, rw_any, dtok_ref, dprob_ref, grad_ref, total_ref, ids_ref, rw_ref, sem):
     tok, width = dtok_ref.shape
     grad_copy = pltpu.make_async_copy(halves_ref, grad_ref, sem.at[0])
     total_copy = pltpu.make_async_copy(total_any, total_ref, sem.at[1])
-    total_copy.start()
-    grad_copy.start()
+    ids_copy = pltpu.make_async_copy(ids_any, ids_ref, sem.at[2])
+    rw_copy = pltpu.make_async_copy(rw_any, rw_ref, sem.at[3])
+    for copy in (ids_copy, rw_copy, total_copy, grad_copy):
+        copy.start()
     total_copy.wait()
     dtok_ref[...] = total_ref[:, 0:width].astype(BF16)
     probs = total_ref[:, width:width + LANES].astype(BF16)
@@ -371,6 +394,8 @@
     other = lax.broadcasted_iota(jnp.int32, (LANES, LANES), 1)
     same = jnp.where(name == other, 1.0, 0.0).astype(BF16)
     probs = dot_t(same, probs)
+    ids_copy.wait()
+    rw_copy.wait()
     name = lax.broadcasted_iota(jnp.int32, (LANES, tok), 0)
     slot = lax.broadcasted_iota(jnp.int32, (4, tok), 0)
     values = jnp.zeros((4, tok), F32)
@@ -403,7 +428,7 @@
             jax.ShapeDtypeStruct((tok, wide), F32),
             jax.ShapeDtypeStruct((2, half_hid, width), F32),
         ),
-        in_specs=[hbm, hbm, vmem, vmem, hbm, hbm, hbm],
+        in_specs=[hbm] * 7,
         out_specs=(vmem, vmem),
         scratch_shapes=[
             pltpu.VMEM((tok, LANES), BF16),
@@ -430,15 +455,17 @@
             pltpu.VMEM((nx, half_hid, width), BF16),
             pltpu.VMEM((half_hid, width), F32),
             pltpu.VMEM((half_hid, width), F32),
-            pltpu.SemaphoreType.DMA((192,)),
-            pltpu.SemaphoreType.DMA((192,)),
-            pltpu.SemaphoreType.DMA((8,)),
+            pltpu.VMEM((4, tok), jnp.int32),
+            pltpu.VMEM((4, tok), BF16),
+            pltpu.SemaphoreType.DMA((256,)),
+            pltpu.SemaphoreType.DMA((256,)),
+            pltpu.SemaphoreType.DMA((10,)),
         ],
         compiler_params=pltpu.CompilerParams(
             collective_id=0, has_side_effects=True, vmem_limit_bytes=48 << 20
         ),
     )(
-        stay(tokens), stay(upstream), ids, scales,
+        stay(tokens), stay(upstream), stay(ids), stay(scales),
         stay(gate_weight[0]), stay(up_weight[0]), stay(down_weight[0]),
     )
     d_tokens, d_probs, grad = pl.pallas_call(
@@ -448,11 +475,14 @@
             jax.ShapeDtypeStruct((4, tok), BF16),
             jax.ShapeDtypeStruct((2, half_hid, width), F32),
         ),
-        in_specs=[anywhere, anywhere, vmem, vmem],
+        in_specs=[anywhere, anywhere, hbm, hbm],
         out_specs=(vmem, vmem, anywhere),
-        scratch_shapes=[pltpu.VMEM((tok, wide), F32), pltpu.SemaphoreType.DMA((2,))],
+        scratch_shapes=[
+            pltpu.VMEM((tok, wide), F32), pltpu.VMEM((4, tok), jnp.int32),
+            pltpu.VMEM((4, tok), BF16), pltpu.SemaphoreType.DMA((4,)),
+        ],
         compiler_params=pltpu.CompilerParams(vmem_limit_bytes=8 << 20),
-    )(total, halves, ids, scales)
+    )(total, halves, stay(ids), stay(scales))
     return d_tokens, d_probs.T, grad.reshape(1, hid, width)
 
 

time: 112 us -> 108 us (0.964)
  Pallas kernels: 110 us -> 108 us
    pallas_call x1, Pallas kernels: 109 us -> 106 us  [local(): pl.pallas_call(functools.partial(kernel, sizes), out_shape=(jax.ShapeDtyp...]
where the time goes in v3:
time: 108 us
  Pallas kernels  108 us (100%)
    pallas_call x1, Pallas kernels, local(): pl.pallas_call(functools.partial(kernel, sizes), out_shape=(jax.ShapeDtyp...  106 us

profile of v3, /device:TPU:2, one launch (start us, length us, event | category | flops | bytes accessed | tf_op | source)
XLA Modules:
  0.0 108.3 jit_solution(1752451706667523732)
XLA Ops:
  0.6 106.0 %shard_map.94 = (f32[32,2176]{1,0:T(8,128)S(1)}, f32[2,48,2048]{2,1,0:T(8,128)S(1)}) custom-call(bf16[32,2048]{1,0:T(8,128)(2,1)} %tok_ref.1, bf16[32,2048]{1,0:T(8,128)(2,1)} %ups_ref.1, s32[4,32]{1,0:T(4,128)} %bitcast.10, bf16[4,32]{1,0:T(4,128)(2,1)} %bitcast.12, bf16[96,2048]{1,0:T(8,128)(2,1)} %bitcast.7, bf16[96,2048]{1,0:T(8,128)(2,1)} %bitcast.8, ...), custom_call_target="tpu_custom_call" | custom-call | tf_op jit(solution)/shard_map/pallas_call | solution.py:425
  106.7 1.6 %shard_map.95 = (bf16[32,2048]{1,0:T(8,128)(2,1)}, bf16[4,32]{1,0:T(4,128)(2,1)}, f32[2,48,2048]{2,1,0:T(8,128)}) custom-call(f32[32,2176]{1,0:T(8,128)S(1)} %get-tuple-element.8.total_any, f32[2,48,2048]{2,1,0:T(8,128)S(1)} %get-tuple-element.9.halves_ref, s32[4,32]{1,0:T(4,128)} %bitcast.11, bf16[4,32]{1,0:T(4,128)(2,1)} %bitcast.13), custom_call_target="tpu_custom_call" | custom-call | tf_op jit(solution)/shard_map/pallas_call | solution.py:471

commit v4 on v3

--- a/solution.py
+++ b/solution.py
@@ -31,17 +31,20 @@
     total_ref, grad_ref,
     meta, xa, dya, seltr, stage, rows, weights, act, dgate, dup, dxs, ret, part,
     fsend, frecv, bsend, brecv, gacc, gsend, gpart, ssend, srecv, gfin, gother,
-    ids_own, rw_own, send_sem, recv_sem, local_sem,
+    ids_own, rw_own, spsend, sprecv, lbuf, spread_in, dxq, dxe, pack7, pack8,
+    rsend7, rsend8, rrecv7, rrecv8, take7, take8, send_sem, recv_sem, local_sem,
 ):
     nx, ny, nz = sizes
     tok, width = tok_ref.shape
     hid = gate_ref.shape[0]
     half_hid = hid // 2
     hidden = nx * hid
-    half = nz // 2
+    near = nz // 2 - 2
     batches = nz // 4
-    pairs = nz // 2
+    last = batches - 1
+    own = 2 * near
     wide = width + LANES
+    quarter = width // 4
     core, ep, dp = lax.axis_index("rep"), lax.axis_index("ep"), lax.axis_index("dp")
     z, y = ep // ny, lax.rem(ep, ny)
 
@@ -56,12 +59,13 @@
 
     partner = (1 - core, ep, dp)
 
-    order = [0]
-    for step in range(1, half):
+    def at_zy(step, side):
+        return (core, lax.rem(z + step + nz, nz) * ny + lax.rem(y + side, ny), dp)
+
+    order = []
+    for step in range(1, near + 1):
         order += [-step, step]
-    order.append(half)
-    place = {delta: index for index, delta in enumerate(order)}
-    place[-half] = place[half]
+    place = {delta: index for index, delta in enumerate(order + [0])}
 
     started = []
 
@@ -78,7 +82,7 @@
     shard_refs = (gate_ref, up_ref, down_ref)
     mine = pl.ds(pl.multiple_of(core * half_hid, half_hid), half_hid)
     theirs = pl.ds(pl.multiple_of((1 - core) * half_hid, half_hid), half_hid)
-    loads = [(ids_ref, ids_own), (rw_ref, rw_own), (tok_ref, xa.at[0, :, pl.ds(0, width)]), (ups_ref, dya.at[0])]
+    loads = [(ids_ref, ids_own), (rw_ref, rw_own), (tok_ref, xa.at[own, :, pl.ds(0, width)]), (ups_ref, dya.at[own])]
     for index, ref in enumerate(shard_refs):
         loads.append((ref.at[mine], weights.at[index, 0, 0]))
         loads.append((ref.at[theirs], weights.at[index, 0, 1]))
@@ -90,7 +94,7 @@
         copy.start()
 
     barrier = pltpu.get_barrier_semaphore()
-    peers = [at_z(1), at_z(-1), partner]
+    peers = [at_zy(step, side) for step in (-2, -1, 1, 2) for side in range(ny)] + [partner]
     peers += [at_y(step) for step in range(1, ny)]
     peers += [at_x(step) for step in range(1, nx)]
     for peer in peers:
@@ -132,7 +136,7 @@
     first_x(1)
     first_m(1)
     first_d(-1)
-    xa[0, :, width:wide] = own_meta
+    xa[own, :, width:wide] = own_meta
 
     wcopy = {}
     for index, ref in enumerate(shard_refs):
@@ -175,18 +179,20 @@
         slot = (lax.rem(r, CAP) + 1).astype(F32)
         return (value == slot) & (c // tok == lax.rem(r // CAP, sources))
 
-    def picks(size, row_block):
+    def picks(size, row_block, plane=0):
         row = lax.broadcasted_iota(jnp.int32, (size, LANES), 0)
         col = lax.broadcasted_iota(jnp.int32, (size, LANES), 1)
-        expert = z * ny + lax.rem(y + row // row_block, ny)
+        expert = lax.rem(z + plane + nz, nz) * ny + lax.rem(y + row // row_block, ny)
         pick = jnp.where(col == expert, 1.0, 0.0).astype(BF16)
         pick_w = jnp.where(col == expert + 64, 1.0, 0.0).astype(BF16)
         return pick, pick_w
 
     def dispatch(p):
-        group = xa[2 * p:2 * p + 2, :, width:wide].reshape(2 * tok, LANES)
+        low, high = (2 * p, 2 * p + 2) if p < near else (own, own + 1)
+        size_t = (high - low) * tok
+        group = xa[low:high, :, width:wide].reshape(size_t, LANES)
         pick, pick_w = picks(count, block)
-        shape = (count, 2 * tok)
+        shape = (count, size_t)
         r, c = (lax.broadcasted_iota(jnp.int32, shape, axis) for axis in (0, 1))
         hit = chosen(dot_t(pick, group), r, c, 2)
         sel = jnp.where(hit, 1.0, 0.0).astype(BF16)
@@ -194,7 +200,7 @@
         for start, size in tiles(width):
             parts = []
             for source, chooser in ((xa, sel), (dya, sel_w)):
-                value = source[2 * p:2 * p + 2, :, start:start + size].reshape(2 * tok, size)
+                value = source[low:high, :, start:start + size].reshape(size_t, size)
                 parts.append(dot_n(chooser, value).reshape(ny, block, size))
             out = jnp.concatenate(parts, axis=1).astype(BF16)
             rows[p, 0, :, start:start + size] = out[0]
@@ -202,6 +208,104 @@
         for step in range(1, ny):
             ycopy[p, step] = send(stage.at[p, step], rows.at[p, ny - step], at_y(step))
 
+    spcopy = []
+
+    def special(sign, kind, planes):
+        source = (xa, dya)[kind]
+        index = place[sign * near]
+        group = xa[index, :, width:wide]
+        group = jnp.concatenate([group] * 4, axis=0)
+        value = jnp.concatenate(
+            [source[index, :, quarter * q:quarter * (q + 1)] for q in range(4)], axis=0
+        )
+        for plane in planes:
+            pick, pick_w = picks(2 * count, 2 * block, plane)
+            shape = (2 * count, 4 * tok)
+            r, c = (lax.broadcasted_iota(jnp.int32, shape, axis) for axis in (0, 1))
+            hit = chosen(dot_t(pick, group), r, c, 4)
+            sel = jnp.where(hit, dot_t(pick_w, group) if kind else 1.0, 0.0).astype(BF16)
+            slot = {1: 0, -1: 1}.get(plane, 2)
+            spsend[slot, kind] = dot_n(sel, value).astype(BF16).reshape(ny, 2 * block, quarter)
+            for side in range(ny):
+                spcopy.append(send(
+                    spsend.at[slot, kind, side], sprecv.at[slot, kind, (ny - side) % ny], at_zy(plane, side)
+                ))
+
+    def digits(shape, axis, *sizes):
+        value = lax.broadcasted_iota(jnp.int32, shape, axis)
+        found = []
+        for size in reversed(sizes):
+            found.append(lax.rem(value, size))
+            value = value // size
+        return found[::-1]
+
+    def constants():
+        shape = (4 * count, 6 * 2 * count)
+        rb, ry, rk, rj, rs = digits(shape, 0, 2, ny, 2, 2, CAP)
+        ci, ck, cy, cq, cs = digits(shape, 1, 3, 2, ny, 4, CAP)
+        wanted = jnp.where(rb == 1, rj, 3 * rj - 1)
+        match = (ci == wanted) & (ck == rk) & (cy == ry) & (cs == rs)
+        for q in range(4):
+            spread_in[q] = jnp.where(match & (cq == q), 1.0, 0.0).astype(BF16)
+
+    def more_constants():
+        shape = (4 * count, 8 * count)
+        ri, ry, rq, rs = digits(shape, 0, 2, ny, 4, CAP)
+        cq, cb, cy, cj, cs = digits(shape, 1, 4, 2, ny, 2, CAP)
+        match = (cb == 1) & (cj == ri) & (cq == rq) & (cy == ry) & (cs == rs)
+        pack7[...] = jnp.where(match, 1.0, 0.0).astype(BF16)
+        shape = (2 * count, 8 * count)
+        ri, ry, rq, rs = digits(shape, 0, 2, ny, 2, CAP)
+        cq, cb, cy, cj, cs = digits(shape, 1, 4, 2, ny, 2, CAP)
+        match = (cb == 0) & (cj == 1) & (cq == 2 * rq + ri) & (cy == ry) & (cs == rs)
+        pack8[...] = jnp.where(match, 1.0, 0.0).astype(BF16)
+
+    def takes():
+        for side, sign in ((0, 1), (1, -1)):
+            group = xa[place[sign * near], :, width:wide]
+            pick, _ = picks(2 * count, 2 * block, -sign)
+            shape = (tok, 2 * count)
+            _, cq, cs = digits(shape, 1, ny, 4, CAP)
+            hit = dot_t(group, pick) == (cs + 1).astype(F32)
+            for q in range(4):
+                take7[side, q] = jnp.where(hit & (cq == q), 1.0, 0.0).astype(BF16)
+            pick, _ = picks(count, block, -2 * sign)
+            shape = (tok, count)
+            _, cq, cs = digits(shape, 1, ny, 2, CAP)
+            hit = dot_t(group, pick) == (cs + 1).astype(F32)
+            for q in range(2):
+                take8[side, q] = jnp.where(hit & (cq == q), 1.0, 0.0).astype(BF16)
+
+    def gather_last():
+        for step in range(1, ny):
+            ycopy[near, step].wait_recv()
+        for copy in spcopy:
+            copy.wait_recv()
+        value = sprecv[...].reshape(12 * count, quarter)
+        for q in range(4):
+            out = dot_n(spread_in[q], value)
+            base = rows[near, :, :, quarter * q:quarter * (q + 1)].reshape(2 * count, quarter).astype(F32)
+            lbuf[0:2 * count, quarter * q:quarter * (q + 1)] = (out[0:2 * count] + base).astype(BF16)
+            lbuf[2 * count:4 * count, quarter * q:quarter * (q + 1)] = out[2 * count:4 * count].astype(BF16)
+
+    pcopy = []
+
+    def give_far():
+        value = dxq[...].reshape(8 * count, quarter)
+        out7 = dot_n(pack7[...], value).astype(BF16).reshape(2, ny, 2 * block, quarter)
+        out8 = dot_n(pack8[...], value).astype(BF16).reshape(2, ny, block, quarter)
+        rsend7[:, :, :, 0:quarter] = out7
+        rsend8[:, :, :, 0:quarter] = out8
+        extra = dxe[...]
+        extra = jnp.concatenate([jnp.zeros_like(extra)] * 3 + [extra], axis=0)
+        rsend7[:, :, :, quarter:] = dot_n(pack7[...], extra).astype(BF16).reshape(2, ny, 2 * block, LANES)
+        rsend8[:, :, :, quarter:] = dot_n(pack8[...], extra).astype(BF16).reshape(2, ny, block, LANES)
+        for way, sign in ((0, 1), (1, -1)):
+            for side in range(ny):
+                there = (ny - side) % ny
+                pcopy.append(send(rsend7.at[1 - way, side], rrecv7.at[way, there], at_zy(sign, side)))
+                pcopy.append(send(rsend8.at[way, side], rrecv8.at[way, there], at_zy(2 * sign, side)))
+
     rcopy = {}
     edges = [(width // 4 * c, width // 4 if c < 3 else wide - width // 4 * 3) for c in range(4)]
     cols = [pl.ds(start, size) for start, size in edges]
@@ -211,10 +315,13 @@
         return value[:, 0], value[:, 1]
 
     def forward(b):
-        for p in (2 * b, 2 * b + 1):
-            for step in range(1, ny):
-                ycopy[p, step].wait_recv()
-        both = rows[2 * b:2 * b + 2].reshape(4 * count, width)
+        if b < last:
+            for p in (2 * b, 2 * b + 1):
+                for step in range(1, ny):
+                    ycopy[p, step].wait_recv()
+            both = rows[2 * b:2 * b + 2].reshape(4 * count, width)
+        else:
+            both = lbuf[...]
         gate_pre, _ = split(dot_t(both, weights[0].reshape(hidden, width)))
         up_pre, _ = split(dot_t(both, weights[1].reshape(hidden, width)))
         _, d_act = split(dot_t(both, weights[2].reshape(hidden, width)))
@@ -230,6 +337,11 @@
         give(b, width, LANES, jnp.where(here, prob, 0.0))
 
     def give(b, start, size, value):
+        if b == last:
+            if size == LANES:
+                dxe[...] = value.reshape(2 * count, size).astype(BF16)
+            else:
+                dxq[start // quarter] = value.reshape(2 * count, size).astype(BF16)
         value = value.reshape(2, ny, block, size)
         value = jnp.concatenate([value[0], value[1]], axis=1).astype(BF16)
         dxs[b, 1:ny, :, start:start + size] = value[1:ny]
@@ -238,25 +350,23 @@
     def backward(b):
         d_gate, d_up = dgate[...], dup[...]
         for col in range(4):
-            start, size = width // 4 * col, width // 4
+            start, size = quarter * col, quarter
             gate_t = weights[0, :, :, :, start:start + size].reshape(hidden, size)
             up_t = weights[1, :, :, :, start:start + size].reshape(hidden, size)
             give(b, start, size, dot_n(d_gate, gate_t) + dot_n(d_up, up_t))
-            if b == batches - 1:
-                for step in range(1, ny):
-                    rcopy[b, col, step] = send(
-                        dxs.at[b, step, :, cols[col]], ret.at[b, ny - step, :, cols[col]], at_y(step)
-                    )
-        if b < batches - 1:
-            for step in range(1, ny):
-                rcopy[b, 0, step] = send(dxs.at[b, step], ret.at[b, ny - step], at_y(step))
+        if b == last:
+            give_far()
+        for step in range(1, ny):
+            rcopy[b, 0, step] = send(dxs.at[b, step], ret.at[b, ny - step], at_y(step))
 
     def spread(b):
-        group = xa[4 * b:4 * b + 4, :, width:wide].reshape(4 * tok, LANES)
+        low, high = (4 * b, 4 * b + 4) if b < last else (own, own + 1)
+        size_t = (high - low) * tok
+        group = xa[low:high, :, width:wide].reshape(size_t, LANES)
         pick, _ = picks(2 * count, 2 * block)
-        shape = (4 * tok, 2 * count)
+        shape = (size_t, 2 * count)
         c, r = (lax.broadcasted_iota(jnp.int32, shape, axis) for axis in (0, 1))
-        seltr[b] = jnp.where(chosen(dot_t(group, pick), r, c, 4), 1.0, 0.0).astype(BF16)
+        seltr[b, 0:size_t] = jnp.where(chosen(dot_t(group, pick), r, c, 4), 1.0, 0.0).astype(BF16)
 
     def combine(b, col):
         if (b, col, ny - 1) in rcopy:
@@ -264,12 +374,18 @@
                 rcopy[b, col, step].wait_recv()
         start, size = edges[col]
         value = ret[b, :, :, start:start + size].reshape(2 * count, size)
-        part[4 * b:4 * b + 4, :, start:start + size] = dot_n(seltr[b], value).reshape(4, tok, size)
+        if b < last:
+            part[4 * b:4 * b + 4, :, start:start + size] = dot_n(seltr[b], value).reshape(4, tok, size)
+        else:
+            part[own, :, start:start + size] = dot_n(seltr[b, 0:tok], value)
 
     def grads(b):
         act_t = act[b].T
         for start, size in tiles(width):
-            value = rows[2 * b:2 * b + 2, :, :, start:start + size].reshape(4 * count, size)
+            if b < last:
+                value = rows[2 * b:2 * b + 2, :, :, start:start + size].reshape(4 * count, size)
+            else:
+                value = lbuf[:, start:start + size]
             out = dot_n(act_t, value).reshape(nx, 2, half_hid, size)
             if b:
                 out = out + gacc[:, :, :, start:start + size]
@@ -277,50 +393,51 @@
             if b == batches - 1:
                 gsend[:, :, start:start + size] = out[:, 1].astype(BF16)
 
-    if half == 8:
-        table = {
-            4: [near_weights], 8: [far_weights], 9: [all_weights],
-            10: [lambda: forward(0)], 11: [lambda: backward(0)],
-            12: [lambda: forward(1)], 13: [lambda: backward(1)],
-            14: [lambda: grads(0)], 15: [lambda: grads(1)],
-            17: [lambda: forward(2), lambda: backward(2), lambda: grads(2)],
-        }
-    else:
-        table = {2 * half + 1: [near_weights, far_weights, all_weights]}
-        for b in range(batches - 1):
-            table[2 * half + 1] += [
-                functools.partial(forward, b), functools.partial(backward, b), functools.partial(grads, b)
-            ]
-
-    for step in range(1, half + 1):
+    table = {
+        2: [lambda: dispatch(near)], 4: [near_weights], 5: [constants], 7: [more_constants],
+        8: [far_weights], 9: [all_weights, lambda: forward(0)],
+        10: [lambda: backward(0)], 11: [lambda: forward(1)],
+        12: [lambda: special(-1, 0, (2, 1)), lambda: backward(1)],
+        13: [lambda: special(1, 1, (-2, -1)), lambda: special(1, 0, (-1,)), lambda: special(-1, 1, (1,))],
+    }
+
+    for step in range(1, near + 1):
         for slot, routes in (
-            (2 * step, ((xa, xcopy, -1, half), (dya, dcopy, 1, half))),
-            (2 * step + 1, ((dya, dcopy, -1, half - 1), (xa, xcopy, 1, half - 1))),
+            (2 * step, ((xa, xcopy, -1), (dya, dcopy, 1))),
+            (2 * step + 1, ((dya, dcopy, -1), (xa, xcopy, 1))),
         ):
-            for moving, copies, sign, last in routes:
-                if step <= last:
-                    copies[sign * step].wait_recv()
-                    if step == 1 and moving is xa:
-                        mcopy[sign].wait_recv()
-                    if step < last:
-                        copies[sign * (step + 1)] = send(
-                            moving.at[place[sign * step]], moving.at[place[sign * (step + 1)]], at_z(-sign)
-                        )
+            for moving, copies, sign in routes:
+                copies[sign * step].wait_recv()
+                if step == 1 and moving is xa:
+                    mcopy[sign].wait_recv()
+                if step < near:
+                    copies[sign * (step + 1)] = send(
+                        moving.at[place[sign * step]], moving.at[place[sign * (step + 1)]], at_z(-sign)
+                    )
+            for task in table.get(slot, ()):
+                task()
             if slot == 2 * step + 1:
                 dispatch(step - 1)
-            for task in table.get(slot, ()):
-                task()
-
-    last = batches - 1
+
+    takes()
+    grads(0)
+    grads(1)
+    spread(0)
+    spread(1)
+    forward(2)
+    backward(2)
+    gather_last()
     forward(last)
     backward(last)
-    grads(last)
+    for b in range(2, batches):
+        grads(b)
     gcopy = send(gsend, gpart, partner)
     for b in range(batches):
-        spread(b)
-    for b in range(batches - 1):
-        for col in range(4):
-            combine(b, col)
+        if b > 1:
+            spread(b)
+        if b < last:
+            for col in range(4):
+                combine(b, col)
 
     def pair_sum():
         gcopy.wait_recv()
@@ -337,7 +454,14 @@
     def relay(col, sign, dist):
         sends, recvs = (fsend, frecv) if sign == 1 else (bsend, brecv)
         value = part[place[sign * dist], :, cols[col]]
-        if (col, sign, dist) in chain:
+        if dist == near:
+            way, size = (1 - sign) // 2, edges[col][1]
+            far = rrecv7[way, :, :, 0:size].reshape(2 * count, size)
+            value = value + dot_n(take7[way, col], far)
+            if col % 2 == way:
+                far = rrecv8[way, :, :, 0:size].reshape(count, size)
+                value = value + dot_n(take8[way, col // 2], far)
+        else:
             chain[col, sign, dist].wait_recv()
             value = value + recvs[dist, :, cols[col]].astype(F32)
         sends[dist, :, cols[col]] = value.astype(BF16)
@@ -345,17 +469,17 @@
             sends.at[dist, :, cols[col]], recvs.at[dist - 1, :, cols[col]], at_z(sign)
         )
 
-    for turn in range(half):
+    for copy in pcopy:
+        copy.wait_recv()
+    for turn in range(near):
         for col in range(4):
-            if turn == 0:
-                combine(last, col)
-            long = 1 if col % 2 == 0 else -1
-            relay(col, long, half - turn)
-            if turn < half - 1:
-                relay(col, -long, half - 1 - turn)
+            relay(col, 1, near - turn)
+            relay(col, -1, near - turn)
         if turn == 0:
             scopy = pair_sum()
-        if turn == max(0, half - 3):
+            for col in range(4):
+                combine(last, col)
+        if turn == near - 2:
             total = gacc[0, 0]
             for rel in range(1, nx):
                 scopy[rel - 1].wait_recv()
@@ -371,7 +495,7 @@
         chain[col, -1, 0].wait_recv()
         start, size = edges[col]
         total_ref[:, start:start + size] = (
-            part[0, :, start:start + size]
+            part[own, :, start:start + size]
             + frecv[0, :, start:start + size].astype(F32)
             + brecv[0, :, start:start + size].astype(F32)
         )
@@ -412,7 +536,7 @@
     hid = gate_weight.shape[1]
     half_hid, hidden = hid // 2, hid * nx
     half, batches = nz // 2, nz // 4
-    wide, block = width + LANES, 4 * CAP
+    wide, block, quarter = width + LANES, 4 * CAP, width // 4
     count = ny * block
     vmem = pl.BlockSpec(memory_space=pltpu.VMEM)
     hbm = pl.BlockSpec(memory_space=pltpu.HBM)
@@ -457,6 +581,20 @@
             pltpu.VMEM((half_hid, width), F32),
             pltpu.VMEM((4, tok), jnp.int32),
             pltpu.VMEM((4, tok), BF16),
+            pltpu.VMEM((3, 2, ny, block, quarter), BF16),
+            pltpu.VMEM((3, 2, ny, block, quarter), BF16),
+            pltpu.VMEM((2 * count, width), BF16),
+            pltpu.VMEM((4, 2 * count, 6 * count), BF16),
+            pltpu.VMEM((4, count, quarter), BF16),
+            pltpu.VMEM((count, LANES), BF16),
+            pltpu.VMEM((2 * count, 4 * count), BF16),
+            pltpu.VMEM((count, 4 * count), BF16),
+            pltpu.VMEM((2, ny, block, quarter + LANES), BF16),
+            pltpu.VMEM((2, ny, block // 2, quarter + LANES), BF16),
+            pltpu.VMEM((2, ny, block, quarter + LANES), BF16),
+            pltpu.VMEM((2, ny, block // 2, quarter + LANES), BF16),
+            pltpu.VMEM((2, 4, tok, count), BF16),
+            pltpu.VMEM((2, 2, tok, count // 2), BF16),
             pltpu.SemaphoreType.DMA((256,)),
             pltpu.SemaphoreType.DMA((256,)),
             pltpu.SemaphoreType.DMA((10,)),

time: 108 us -> 105 us (0.972)
  the two profiles are of different devices: /device:TPU:2 before, /device:TPU:32 now
where the time goes in v4:
time: 105 us
  Pallas kernels  104 us (99%)
    pallas_call x1, Pallas kernels, local(): pl.pallas_call(functools.partial(kernel, sizes), out_shape=(jax.ShapeDtyp...  103 us

profile of v4, /device:TPU:32, one launch (start us, length us, event | category | flops | bytes accessed | tf_op | source)
XLA Modules:
  0.0 105.0 jit_solution(4646105221074892703)
XLA Ops:
  0.6 102.8 %shard_map.94 = (f32[32,2176]{1,0:T(8,128)S(1)}, f32[2,48,2048]{2,1,0:T(8,128)S(1)}) custom-call(bf16[32,2048]{1,0:T(8,128)(2,1)} %tok_ref.1, bf16[32,2048]{1,0:T(8,128)(2,1)} %ups_ref.1, s32[4,32]{1,0:T(4,128)} %bitcast.10, bf16[4,32]{1,0:T(4,128)(2,1)} %bitcast.12, bf16[96,2048]{1,0:T(8,128)(2,1)} %bitcast.7, bf16[96,2048]{1,0:T(8,128)(2,1)} %bitcast.8, ...), custom_call_target="tpu_custom_call" | custom-call | tf_op jit(solution)/shard_map/pallas_call | solution.py:549
  103.4 1.6 %shard_map.95 = (bf16[32,2048]{1,0:T(8,128)(2,1)}, bf16[4,32]{1,0:T(4,128)(2,1)}, f32[2,48,2048]{2,1,0:T(8,128)}) custom-call(f32[32,2176]{1,0:T(8,128)S(1)} %get-tuple-element.8.total_any, f32[2,48,2048]{2,1,0:T(8,128)S(1)} %get-tuple-element.9.halves_ref, s32[4,32]{1,0:T(4,128)} %bitcast.11, bf16[4,32]{1,0:T(4,128)(2,1)} %bitcast.13), custom_call_target="tpu_custom_call" | custom-call | tf_op jit(solution)/shard_map/pallas_call | solution.py:609

commit v5 on v4

--- a/solution.py
+++ b/solution.py
@@ -354,10 +354,16 @@
             gate_t = weights[0, :, :, :, start:start + size].reshape(hidden, size)
             up_t = weights[1, :, :, :, start:start + size].reshape(hidden, size)
             give(b, start, size, dot_n(d_gate, gate_t) + dot_n(d_up, up_t))
+            if b == last - 1:
+                for step in range(1, ny):
+                    rcopy[b, col, step] = send(
+                        dxs.at[b, step, :, cols[col]], ret.at[b, ny - step, :, cols[col]], at_y(step)
+                    )
         if b == last:
             give_far()
-        for step in range(1, ny):
-            rcopy[b, 0, step] = send(dxs.at[b, step], ret.at[b, ny - step], at_y(step))
+        if b != last - 1:
+            for step in range(1, ny):
+                rcopy[b, 0, step] = send(dxs.at[b, step], ret.at[b, ny - step], at_y(step))
 
     def spread(b):
         low, high = (4 * b, 4 * b + 4) if b < last else (own, own + 1)
@@ -424,18 +430,19 @@
     grads(1)
     spread(0)
     spread(1)
-    forward(2)
-    backward(2)
+    spread(2)
     gather_last()
     forward(last)
     backward(last)
+    forward(2)
+    backward(2)
     for b in range(2, batches):
         grads(b)
     gcopy = send(gsend, gpart, partner)
     for b in range(batches):
-        if b > 1:
+        if b == last:
             spread(b)
-        if b < last:
+        if b < last - 1:
             for col in range(4):
                 combine(b, col)
 
@@ -473,6 +480,8 @@
         copy.wait_recv()
     for turn in range(near):
         for col in range(4):
+            if turn == 0:
+                combine(last - 1, col)
             relay(col, 1, near - turn)
             relay(col, -1, near - turn)
         if turn == 0:

time: 105 us -> 104 us (level)
  no operation moved by 1% of the time
where the time goes in v5:
time: 104 us
  Pallas kernels  103 us (99%)
    pallas_call x1, Pallas kernels, local(): pl.pallas_call(functools.partial(kernel, sizes), out_shape=(jax.ShapeDtyp...  102 us

profile of v5, /device:TPU:32, one launch (start us, length us, event | category | flops | bytes accessed | tf_op | source)
XLA Modules:
  0.0 104.1 jit_solution(5755564979523052767)
XLA Ops:
  0.6 101.9 %shard_map.94 = (f32[32,2176]{1,0:T(8,128)S(1)}, f32[2,48,2048]{2,1,0:T(8,128)S(1)}) custom-call(bf16[32,2048]{1,0:T(8,128)(2,1)} %tok_ref.1, bf16[32,2048]{1,0:T(8,128)(2,1)} %ups_ref.1, s32[4,32]{1,0:T(4,128)} %bitcast.10, bf16[4,32]{1,0:T(4,128)(2,1)} %bitcast.12, bf16[96,2048]{1,0:T(8,128)(2,1)} %bitcast.7, bf16[96,2048]{1,0:T(8,128)(2,1)} %bitcast.8, ...), custom_call_target="tpu_custom_call" | custom-call | tf_op jit(solution)/shard_map/pallas_call | solution.py:558
  102.5 1.6 %shard_map.95 = (bf16[32,2048]{1,0:T(8,128)(2,1)}, bf16[4,32]{1,0:T(4,128)(2,1)}, f32[2,48,2048]{2,1,0:T(8,128)}) custom-call(f32[32,2176]{1,0:T(8,128)S(1)} %get-tuple-element.8.total_any, f32[2,48,2048]{2,1,0:T(8,128)S(1)} %get-tuple-element.9.halves_ref, s32[4,32]{1,0:T(4,128)} %bitcast.11, bf16[4,32]{1,0:T(4,128)(2,1)} %bitcast.13), custom_call_target="tpu_custom_call" | custom-call | tf_op jit(solution)/shard_map/pallas_call | solution.py:618
